TPU v7x, 256 devices: a whole 4x4x8 slice. The times are simulated.
256 devices in a mesh: ctx: 32 (over y, z), head: 8 (over x, core).
Axes of the slice: x: 4, y: 4, z: 8, core: 2. Of those that a mesh axis runs over, the one named last changes fastest.
Arguments:
- queries: bfloat16 [8192, 4096], P('ctx', 'head'), may hold values from -6 to 6
- key_rows: bfloat16 [8192, 4096], P('ctx', 'head'), may hold values from -0.5 to 0.5
- value_rows: bfloat16 [8192, 4096], P('ctx', 'head'), may hold values from -6 to 6
- doc_ids: int32 [8192], P('ctx'), may hold values from 0 to 15, never falling along the last dimension, each value on 1 to 2048 neighbouring positions
- out_grad: bfloat16 [8192, 6144], P(('ctx', 'head')), may hold values from -6 to 6
- out_weight: bfloat16 [4096, 6144], P('head', 'ctx'), may hold values from -0.09375 to 0.09375
Outputs:
- layer_out: bfloat16 [8192, 6144], P(('ctx', 'head'))
- query_grad: bfloat16 [8192, 4096], P('ctx', 'head')
- key_grad: bfloat16 [8192, 4096], P('ctx', 'head')
- value_grad: bfloat16 [8192, 4096], P('ctx', 'head')
- weight_grad: bfloat16 [4096, 6144], P(('head', 'ctx'))
Inputs may be any that keep to these rules, and one draw needn't show every extreme that they name: `doc_ids`: repository ids never fall along the sequence; each repository covers 1 to 2048 tokens, and one covers exactly that many.
All inputs are finite; a program needn't handle non-finite values.
Results may differ from a plain program's by a relative error of at most 0.025.
Values may be sent and summed in bfloat16 or wider, within the bound.
No kernel may reach another device: no remote copies, remote signals or barrier semaphores. Data moves between devices by JAX's collectives and lax.ppermute only.
A program may use at most 128 MiB of HBM per device.

v0:
```python
import jax
import jax.numpy as jnp
from jax import lax
from jax.sharding import PartitionSpec as P

HD = 128


EPSILON = 1e-05


def carried_in(x, axis, join, neutral, backward):
    count = lax.axis_size(axis)
    place = lax.axis_index(axis)
    ahead = count - 1 - place if backward else place
    gathered = jax.tree.map(
        lambda a, kind: lax.all_gather(a.astype(kind), axis),
        x,
        (jnp.bfloat16, jnp.bfloat16, jnp.bfloat16),
    )
    state = jax.tree.map(lambda a, e: jnp.zeros_like(a) + jnp.asarray(e, a.dtype), x, neutral)

    def one(lap, state):
        source = count - 1 - lap if backward else lap
        return join(
            state,
            jax.tree.map(
                lambda a, own: lax.dynamic_index_in_dim(a, source, 0, False).astype(own.dtype),
                gathered,
                x,
            ),
        )

    return lax.fori_loop(0, ahead, one, state)


def forward_link(earlier_part, later_part):
    early_first, early_last, early_state = earlier_part
    late_first, late_last, late_state = later_part
    late_empty = late_last < 0.0
    early_empty = early_last < 0.0
    linked = (early_last == late_first) & (late_first == late_last)
    joined = late_state + jnp.where(linked, early_state, jnp.float32(0.0))
    return (
        jnp.where(early_empty, late_first, early_first),
        jnp.where(late_empty, early_last, late_last),
        jnp.where(late_empty, early_state, joined),
    )


def backward_link(earlier_part, later_part):
    high_first, high_last, high_state = earlier_part
    low_first, low_last, low_state = later_part
    low_empty = low_last < 0.0
    high_empty = high_last < 0.0
    linked = (high_first == low_last) & (low_first == low_last)
    joined = low_state + jnp.where(linked, high_state, jnp.float32(0.0))
    return (
        jnp.where(low_empty, high_first, low_first),
        jnp.where(high_empty, low_last, high_last),
        jnp.where(low_empty, high_state, joined),
    )


def shards(queries, key_rows, value_rows, doc_ids, out_grad, out_weight):
    tok_count, full_width = queries.shape
    head_count = full_width // HD
    query_heads = queries.reshape(tok_count, head_count, HD)
    key_heads = key_rows.reshape(tok_count, head_count, HD)
    value_heads = value_rows.reshape(tok_count, head_count, HD)
    doc_values = doc_ids.astype(jnp.float32)
    first_doc = doc_values[:1]
    last_doc = doc_values[-1:]
    causal = jnp.tril(jnp.ones((tok_count, tok_count), dtype=bool))
    allowed = (causal & (doc_ids[:, None] == doc_ids[None, :]))[None]
    scores = jnp.einsum("thd,shd->hts", query_heads, key_heads, preferred_element_type=jnp.float32)
    weights = jnp.where(allowed, scores, jnp.float32(0.0)).astype(jnp.bfloat16)
    key_last = jnp.where(
        (doc_values == last_doc)[:, None, None], key_heads, jnp.zeros_like(key_heads)
    )
    local_state = jnp.einsum(
        "thd,the->hde", key_last, value_heads, preferred_element_type=jnp.float32
    )
    empty_marks = jnp.full((1,), -1.0, jnp.float32)
    identity = (empty_marks, empty_marks, jnp.zeros_like(local_state))
    prior_first, prior_last, prior_state = carried_in(
        (first_doc, last_doc, local_state), "ctx", forward_link, identity, False
    )
    row_mask = doc_values == prior_last
    prior_rounded = prior_state.astype(jnp.bfloat16)
    inter = jnp.einsum(
        "thd,hde->the", query_heads, prior_rounded, preferred_element_type=jnp.float32
    )
    mixed = jnp.einsum(
        "hts,she->the", weights, value_heads, preferred_element_type=jnp.float32
    ) + jnp.where(row_mask[:, None, None], inter, jnp.float32(0.0))
    inv_norm = lax.rsqrt(jnp.mean(mixed * mixed, axis=-1, keepdims=True) + EPSILON)
    normed = mixed * inv_norm
    normed_flat = normed.astype(jnp.bfloat16).reshape(tok_count, full_width)
    full_weight = lax.all_gather(out_weight, "ctx", axis=1, tiled=True)
    layer_out = lax.psum_scatter(
        jnp.dot(normed_flat, full_weight, preferred_element_type=jnp.float32).astype(jnp.bfloat16),
        "head",
        scatter_dimension=0,
        tiled=True,
    )
    grad_full = lax.all_gather(out_grad, "head", axis=0, tiled=True)
    grad_normed = lax.dot_general(
        grad_full, full_weight, (((1,), (1,)), ((), ())), preferred_element_type=jnp.float32
    ).reshape(tok_count, head_count, HD)
    mixed_grad = (
        inv_norm * (grad_normed - normed * jnp.mean(grad_normed * normed, axis=-1, keepdims=True))
    ).astype(jnp.bfloat16)
    weight_grad = lax.psum_scatter(
        lax.dot_general(
            normed_flat, grad_full, (((0,), (0,)), ((), ())), preferred_element_type=jnp.float32
        ).astype(jnp.bfloat16),
        "ctx",
        scatter_dimension=0,
        tiled=True,
    )
    query_first = jnp.where(
        (doc_values == first_doc)[:, None, None], query_heads, jnp.zeros_like(query_heads)
    )
    local_future = jnp.einsum(
        "thd,the->hde", query_first, mixed_grad, preferred_element_type=jnp.float32
    )
    later_first, later_last, future_state = carried_in(
        (first_doc, last_doc, local_future), "ctx", backward_link, identity, True
    )
    col_mask = (doc_values == later_first)[:, None, None]
    future_rounded = future_state.astype(jnp.bfloat16)
    grad_raw = jnp.einsum(
        "the,she->hts", mixed_grad, value_heads, preferred_element_type=jnp.float32
    )
    grad_scores = jnp.where(allowed, grad_raw, jnp.float32(0.0)).astype(jnp.bfloat16)
    query_grad = jnp.einsum(
        "hts,shd->thd", grad_scores, key_heads, preferred_element_type=jnp.float32
    ) + jnp.where(
        row_mask[:, None, None],
        jnp.einsum("the,hde->thd", mixed_grad, prior_rounded, preferred_element_type=jnp.float32),
        jnp.float32(0.0),
    )
    key_grad = jnp.einsum(
        "hts,thd->shd", grad_scores, query_heads, preferred_element_type=jnp.float32
    ) + jnp.where(
        col_mask,
        jnp.einsum("she,hde->shd", value_heads, future_rounded, preferred_element_type=jnp.float32),
        jnp.float32(0.0),
    )
    value_grad = jnp.einsum(
        "hts,the->she", weights, mixed_grad, preferred_element_type=jnp.float32
    ) + jnp.where(
        col_mask,
        jnp.einsum("shd,hde->she", key_heads, future_rounded, preferred_element_type=jnp.float32),
        jnp.float32(0.0),
    )
    return (
        layer_out,
        query_grad.astype(jnp.bfloat16).reshape(tok_count, full_width),
        key_grad.astype(jnp.bfloat16).reshape(tok_count, full_width),
        value_grad.astype(jnp.bfloat16).reshape(tok_count, full_width),
        weight_grad,
    )


def solution(mesh):
    return jax.shard_map(
        shards,
        mesh=mesh,
        in_specs=(
            P("ctx", "head"),
            P("ctx", "head"),
            P("ctx", "head"),
            P("ctx"),
            P(("ctx", "head"), None),
            P("head", "ctx"),
        ),
        out_specs=(
            P(("ctx", "head"), None),
            P("ctx", "head"),
            P("ctx", "head"),
            P("ctx", "head"),
            P(("head", "ctx"), None),
        ),
        check_vma=False,
    )
```

profile of v0, /device:TPU:32, one launch (start us, length us, event | category | flops | bytes accessed | tf_op | source)
XLA Modules:
  0.0 607.9 jit_solution(14436302235198908007)
XLA Ops:
  7.9 1.1 copy.86
  9.6 2.0 broadcast_compare_fusion.1
  14.0 1.3 dynamic-slice
  15.9 1.4 dynamic-update-slice
  17.3 1.4 dynamic-update-slice.1
  18.7 74.3 %all-reduce.2 = (bf16[32]{0:T(256)(128)(2,1)S(1)}, bf16[32]{0:T(256)(128)(2,1)S(1)}) all-reduce(bf16[32]{0:T(256)(128)(2,1)S(1)} %dynamic-update-slice, bf16[32]{0:T(256)(128)(2,1)S(1)} %dynamic-update-slice.1), channel_id=2, replica_groups=mesh['ctx'=32,'head'=8] {'ctx'}, use_global_device_ids=true, to_apply=%add | all-reduce | flops 64 | bytes 256
  93.0 1.1 copy.59
  94.9 1.3 fusion.2
  97.3 4.9 while.30
  102.5 23.9 %all-gather.11.cloned.1.call-done = bf16[256,6144]{1,0:T(8,128)(2,1)} async-done(((bf16[32,6144]{1,0:T(8,128)(2,1)}), bf16[256,6144]{1,0:T(8,128)(2,1)}) %all-gather.11.cloned.1.call-update) | async-done | bytes 3145744 | tf_op jit(solution)/shard_map/all_gather | solution.py:107
  126.5 91.0 %all-gather.9.cloned.1.call-done = bf16[512,6144]{0,1:T(8,128)(2,1)} async-done(((bf16[512,192]{0,1:T(8,128)(2,1)}), bf16[512,6144]{0,1:T(8,128)(2,1)}) %all-gather.9.cloned.1.call-update) | async-done | bytes 6291472 | tf_op jit(solution)/shard_map/all_gather | solution.py:100
  217.5 6.3 %multiply_reduce_fusion = (f32[256,4]{0,1:T(4,128)S(1)}, f32[256,512]{0,1:T(8,128)S(1)}) fusion(f32[256,4,128]{0,2,1:T(8,128)S(1)} %get-tuple-element.234, f32[256,4]{0,1:T(4,128)S(1)} %add_rsqrt_fusion, bf16[256,6144]{1,0:T(8,128)(2,1)} %all-gather.11.cloned.1.call-done, bf16[512,6144]{0,1:T(8,128)(2,1)} %all-gather.9.cloned.1.call-done), kind=kOutput, calls=%fused_computation.34 | convolution fusion | flops 1611004928 | bytes 10493952 | tf_op jit(solution)/shard_map/dot_general | solution.py:108
  224.9 6.4 %convolution_convert_fusion.1 = bf16[256,6144]{1,0:T(8,128)(2,1)} fusion(bf16[256,512]{0,1:T(8,128)(2,1)S(1)} %bitcast.132, bf16[512,6144]{0,1:T(8,128)(2,1)} %all-gather.9.cloned.1.call-done), kind=kOutput, calls=%fused_computation.9 | convolution fusion | flops 1612185600 | bytes 9699328 | tf_op jit(solution)/shard_map/dot_general | solution.py:102
  231.4 6.4 %convolution_convert_fusion = bf16[512,6144]{1,0:T(8,128)(2,1)} fusion(bf16[256,512]{0,1:T(8,128)(2,1)S(1)} %bitcast.133, bf16[256,6144]{1,0:T(8,128)(2,1)} %all-gather.11.cloned.1.call-done), kind=kOutput, calls=%fused_computation.8 | convolution fusion | flops 1613758464 | bytes 9699328 | tf_op jit(solution)/shard_map/dot_general | solution.py:115
  239.9 95.6 %all-gather.15.cloned.1.call-done = bf16[128,128,128]{2,1,0:T(8,128)(2,1)} async-done(((bf16[4,128,128]{2,1,0:T(8,128)(2,1)}), bf16[128,128,128]{2,1,0:T(8,128)(2,1)}) %all-gather.15.cloned.1.call-update) | async-done | bytes 4194320 | tf_op jit(solution)/shard_map/all_gather | solution.py:17
  335.5 153.5 %while.31 = (s32[]{:T(128)}, f32[1]{0:T(128)}, f32[4,128,128]{2,1,0:T(8,128)S(1)}, s32[]{:T(128)}, bf16[32,1]{0,1:T(2,128)(2,1)S(1)}, /*index=5*/bf16[32,1]{0,1:...) while((s32[]{:T(128)}, f32[1]{0:T(128)}, ...), condition=%wide.region_6.7_spmd, body=%wide.region_5.6_spmd.sunk | while | flops 262155 | bytes 655590 | solution.py:34
  354.9 1.0 fusion.69
  360.1 1.0 fusion.69
  365.2 1.0 fusion.69
  416.3 1.0 fusion.69
  441.9 1.0 fusion.69
  467.5 1.1 fusion.69
  472.6 1.0 fusion.69
  491.2 109.8 %reduce-scatter.5.cloned.1.call-done = bf16[16,6144]{1,0:T(8,128)(2,1)} async-done(((bf16[512,6144]{1,0:T(8,128)(2,1)}), bf16[16,6144]{1,0:T(8,128)(2,1)}) %reduce-scatter.5.cloned.1.call-update) | async-done | bytes 196624 | tf_op jit(solution)/shard_map/reduce_scatter | solution.py:114
  (102 shorter events, 57.7 us)
Async XLA Ops:
  7.2 4.4 copy-start
  7.2 90.1 %all-gather.13.cloned.1.call-start = ((), (), s32[]{:S(2)}) async-start(), calls=%async_computation.6 | async-start | bytes 4325376 | tf_op jit(solution)/shard_map/all_gather | solution.py:17
  11.6 90.6 %copy-start.2 = (s32[256]{0:T(256)S(1)}, s32[256]{0:T(256)}, u32[]{:S(2)}) copy-start(s32[256]{0:T(256)} %param.13) | copy-start | bytes 3076
  12.5 114.0 %all-gather.11.cloned.1.call-start = ((), (), s32[]{:S(2)}) async-start(), calls=%async_computation.4 | async-start | bytes 3538944 | tf_op jit(solution)/shard_map/all_gather | solution.py:107
  13.2 204.2 %all-gather.9.cloned.1.call-start = ((), (), s32[]{:S(2)}) async-start(), calls=%async_computation.2 | async-start | bytes 6488064 | tf_op jit(solution)/shard_map/all_gather | solution.py:100
  14.0 321.5 %all-gather.15.cloned.1.call-start = ((), (), s32[]{:S(2)}) async-start(), calls=%async_computation.7 | async-start | bytes 4325376 | tf_op jit(solution)/shard_map/all_gather | solution.py:17
  224.8 266.4 %reduce-scatter.3.cloned.1.call-start = ((), (), s32[]{:S(2)}) async-start(), calls=%async_computation.3 | async-start | bytes 3538944 | tf_op jit(solution)/shard_map/reduce_scatter | solution.py:101
  231.3 369.7 %reduce-scatter.5.cloned.1.call-start = ((), (), s32[]{:S(2)}) async-start(), calls=%async_computation.5 | async-start | bytes 6488064 | tf_op jit(solution)/shard_map/reduce_scatter | solution.py:114
  239.5 250.6 %copy-start.1 = (bf16[256,512]{1,0:T(8,128)(2,1)S(1)}, bf16[256,512]{1,0:T(8,128)(2,1)}, u32[]{:S(2)}) copy-start(bf16[256,512]{1,0:T(8,128)(2,1)} %param.11) | copy-start | bytes 786436
Sparse Core Ops, SparseCore 0:
  12.6 84.5 all-gather.12
  99.1 27.3 all-gather.10
  129.0 88.3 all-gather.8
  224.9 110.5 all-gather.14
  338.5 35.3 reduce-scatter.2
  378.3 222.7 reduce-scatter.4
where the time goes:
time: 612 us; the launch traced here: 608 us
  waiting for transfers between devices  322 us (53%)
  loops' own time  105 us (17%)
  blocking collectives  74.3 us (12%)
  other arithmetic  36.1 us (6%)
  local copies, waits for them, and re-layouts  30.7 us (5%)
  matrix products  24.5 us (4%)
  between operations  14.3 us (2%)
    reduce_scatter x1, waiting for transfers between devices, shards(): lax.psum_scatter(lax.dot_general(normed_flat, grad_full, (((0,), (0,)), (...  110 us
    another operation x2, loops' own time, carried_in(): return lax.fori_loop(0, ahead, one, state)  105 us
    all_gather x2, waiting for transfers between devices, carried_in(): lax.all_gather(a.astype(kind), axis)  96.2 us
    all_gather x1, waiting for transfers between devices, shards(): full_weight = lax.all_gather(out_weight, 'ctx', axis=1, tiled=True)  91 us
    unnamed x1, blocking collectives  74.3 us
    select_n x30, other arithmetic, backward_link(): jnp.where(low_empty, high_state, joined)  31.3 us
    all_gather x1, waiting for transfers between devices, shards(): grad_full = lax.all_gather(out_grad, 'head', axis=0, tiled=True)  23.9 us
    dynamic_slice x31, local copies, waits for them, and re-layouts, one(): lax.dynamic_index_in_dim(a, source, 0, False).astype(own.dtype)  20.7 us
  transfers between devices with their start and end apart: 6, of which 5 were waited for; matrix products, arithmetic and copies ran while one was open for 13% of the time, Pallas kernels for 0%

commit v1 on v0

v1 whole, which is shorter than its diff:
```python
import jax
import jax.numpy as jnp
from jax import lax
from jax.sharding import Mesh, PartitionSpec as P

HD = 128
EPSILON = 1e-05
BF = jnp.bfloat16
F32 = jnp.float32
WINDOW = (1, 2, 4)
CTX = ("y", "z")
HEAD = ("x", "c")


def shift(x, by):
    count = lax.axis_size(CTX)
    pairs = [(i, i + by) for i in range(count) if 0 <= i + by < count]
    return lax.ppermute(x, CTX, pairs)


def window_state(local, sent_mark, first_mark, enter_mark, direction):
    rows = local.shape[0]

    def packed(state, mark):
        return jnp.concatenate(
            [state.astype(BF), jnp.full((16, HD), 1.0, BF) * (mark + 1.0).astype(BF)], axis=0
        )

    def opened(message):
        return message[:rows].astype(F32), message[rows, 0].astype(F32) - 1.0

    state, mark = opened(shift(packed(local, sent_mark), direction))
    total = jnp.where(mark == enter_mark, state, 0.0)
    for step in WINDOW:
        state, mark = opened(shift(packed(total, first_mark), direction * step))
        total = total + jnp.where(mark == first_mark, state, 0.0)
    return total


def shards(queries, key_rows, value_rows, doc_ids, out_grad, out_weight):
    tok, width = queries.shape
    heads = width // HD
    ny, nz, nh = lax.axis_size("y"), lax.axis_size("z"), lax.axis_size(HEAD)
    cols = out_grad.shape[1] // ny
    sub = out_grad.shape[0]
    weight_t = lax.all_gather(out_weight.T, "z", axis=0, tiled=True)
    og = lax.all_to_all(out_grad.reshape(sub, ny, cols).transpose(1, 0, 2), "y", 0, 0)
    og = lax.all_gather(og.reshape(ny * sub, cols), HEAD, axis=0, tiled=True)

    query_heads = queries.reshape(tok, heads, HD)
    key_heads = key_rows.reshape(tok, heads, HD)
    value_heads = value_rows.reshape(tok, heads, HD)
    docs = doc_ids.astype(F32)
    first_doc, last_doc = docs[0], docs[-1]
    causal = jnp.tril(jnp.ones((tok, tok), dtype=bool))
    allowed = (causal & (doc_ids[:, None] == doc_ids[None, :]))[None]
    in_first = (docs == first_doc)[:, None, None]
    in_last = (docs == last_doc)[:, None, None]

    key_last = jnp.where(in_last, key_heads, jnp.zeros_like(key_heads))
    local_state = jnp.einsum("thd,the->hde", key_last, value_heads, preferred_element_type=F32)
    prior = window_state(
        local_state.reshape(heads * HD, HD), last_doc, first_doc, first_doc, 1
    ).astype(BF).reshape(heads, HD, HD)

    scores = jnp.einsum("thd,shd->hts", query_heads, key_heads, preferred_element_type=F32)
    weights = jnp.where(allowed, scores, F32(0.0)).astype(BF)
    inter = jnp.einsum("thd,hde->the", query_heads, prior, preferred_element_type=F32)
    mixed = jnp.einsum(
        "hts,she->the", weights, value_heads, preferred_element_type=F32
    ) + jnp.where(in_first, inter, F32(0.0))
    inv_norm = lax.rsqrt(jnp.mean(mixed * mixed, axis=-1, keepdims=True) + EPSILON)
    normed = mixed * inv_norm
    normed_flat = normed.astype(BF).reshape(tok, width)

    gn_part = jnp.dot(og, weight_t, preferred_element_type=F32).astype(BF)
    gn_part = gn_part.reshape(nh, ny, sub, width).transpose(1, 0, 2, 3)
    gn = lax.all_to_all(gn_part, "y", 0, 0)
    grad_normed = jnp.sum(gn.astype(F32), axis=0).reshape(tok, heads, HD)

    normed_all = lax.all_gather(normed_flat.reshape(nh, sub, width), "y", axis=1)
    normed_all = normed_all.reshape(nh * ny * sub, width)
    out_part = lax.dot_general(
        normed_all, weight_t, (((1,), (1,)), ((), ())), preferred_element_type=F32
    ).astype(BF)
    out_sum = lax.psum_scatter(out_part, HEAD, scatter_dimension=0, tiled=True)
    layer_out = lax.all_to_all(out_sum.reshape(ny, sub, cols), "y", 0, 0)
    layer_out = layer_out.transpose(1, 0, 2).reshape(sub, ny * cols)

    wg_part = lax.dot_general(
        normed_all, og, (((0,), (0,)), ((), ())), preferred_element_type=F32
    ).astype(BF)
    rows = width // (ny * nz)
    wg_part = wg_part.reshape(ny, nz, rows, cols).transpose(1, 0, 2, 3).reshape(width, cols)
    wg_sum = lax.psum_scatter(wg_part, "z", scatter_dimension=0, tiled=True)
    wg = lax.all_to_all(wg_sum.reshape(ny, rows, cols), "y", 0, 0)
    weight_grad = wg.transpose(1, 0, 2).reshape(rows, ny * cols)

    mixed_grad = (
        inv_norm * (grad_normed - normed * jnp.mean(grad_normed * normed, axis=-1, keepdims=True))
    ).astype(BF)
    query_first = jnp.where(in_first, query_heads, jnp.zeros_like(query_heads))
    local_future = jnp.einsum("thd,the->hde", query_first, mixed_grad, preferred_element_type=F32)
    future = window_state(
        local_future.reshape(heads * HD, HD), first_doc, last_doc, last_doc, -1
    ).astype(BF).reshape(heads, HD, HD)

    grad_raw = jnp.einsum("the,she->hts", mixed_grad, value_heads, preferred_element_type=F32)
    grad_scores = jnp.where(allowed, grad_raw, F32(0.0)).astype(BF)
    query_grad = jnp.einsum(
        "hts,shd->thd", grad_scores, key_heads, preferred_element_type=F32
    ) + jnp.where(
        in_first,
        jnp.einsum("the,hde->thd", mixed_grad, prior, preferred_element_type=F32),
        F32(0.0),
    )
    key_grad = jnp.einsum(
        "hts,thd->shd", grad_scores, query_heads, preferred_element_type=F32
    ) + jnp.where(
        in_last,
        jnp.einsum("she,hde->shd", value_heads, future, preferred_element_type=F32),
        F32(0.0),
    )
    value_grad = jnp.einsum(
        "hts,the->she", weights, mixed_grad, preferred_element_type=F32
    ) + jnp.where(
        in_last,
        jnp.einsum("shd,hde->she", key_heads, future, preferred_element_type=F32),
        F32(0.0),
    )
    return (
        layer_out,
        query_grad.astype(BF).reshape(tok, width),
        key_grad.astype(BF).reshape(tok, width),
        value_grad.astype(BF).reshape(tok, width),
        weight_grad,
    )


def solution(mesh):
    grid = Mesh(mesh.devices.reshape(4, 8, 4, 2), ("y", "z", "x", "c"))
    return jax.shard_map(
        shards,
        mesh=grid,
        in_specs=(
            P(CTX, HEAD),
            P(CTX, HEAD),
            P(CTX, HEAD),
            P(CTX),
            P(CTX + HEAD, None),
            P(HEAD, CTX),
        ),
        out_specs=(
            P(CTX + HEAD, None),
            P(CTX, HEAD),
            P(CTX, HEAD),
            P(CTX, HEAD),
            P(HEAD + CTX, None),
        ),
        check_vma=False,
    )
```

time: 612 us -> 247 us (0.40)
  waiting for transfers between devices: 322 us -> 125 us
  loops' own time: 105 us -> 0 us
  blocking collectives: 74.3 us -> 12.4 us
  starting transfers between devices: 0.24 us -> 46.6 us
  other arithmetic: 36.1 us -> 3.25 us
  local copies, waits for them, and re-layouts: 30.7 us -> 17 us
  between operations: 14.3 us -> 26 us
  matrix products: 24.5 us -> 15.9 us
    all_gather x4 -> x3, waiting for transfers between devices: 211 us -> 38.1 us  [the longest x1 24.9 us: shards(): lax.all_gather(normed_flat.reshape(nh, sub, width), 'y', axis=1)]
    another operation x2 -> x0, loops' own time: 105 us -> none  [carried_in(): return lax.fori_loop(0, ahead, one, state)]
    reduce_scatter x2, waiting for transfers between devices: 110 us -> 19.2 us  [the longest x1 19.2 us: shards(): out_sum = lax.psum_scatter(out_part, HEAD, scatter_dimension=0, tiled=True)]
    unnamed x1 -> x0, blocking collectives: 74.3 us -> none
    ppermute x0 -> x8, waiting for transfers between devices: none -> 44.7 us  [shift(): return lax.ppermute(x, CTX, pairs)]
    select_n x31 -> x0, other arithmetic: 32.4 us -> none  [the longest x30 31.3 us: backward_link(): jnp.where(low_empty, high_state, joined)]
    ppermute x0 -> x8, starting transfers between devices: none -> 32.4 us  [shift(): return lax.ppermute(x, CTX, pairs)]
    all_to_all x0 -> x3, waiting for transfers between devices: none -> 22.1 us  [the longest x1 11.3 us: shards(): gn = lax.all_to_all(gn_part, 'y', 0, 0)]
  transfers between devices with their start and end apart: 6 -> 16, of which waited for: 5 -> 13; matrix products, arithmetic and copies ran while one was open for 13% -> 11% of each run, Pallas kernels for 0% -> 0%
where the time goes in v1:
time: 247 us; the launch traced here: 246 us
  waiting for transfers between devices  125 us (51%)
  starting transfers between devices  46.6 us (19%)
  between operations  26 us (11%)
  local copies, waits for them, and re-layouts  17 us (7%)
  matrix products  15.9 us (6%)
  blocking collectives  12.4 us (5%)
  other arithmetic  3.25 us (1%)
    ppermute x8, waiting for transfers between devices, shift(): return lax.ppermute(x, CTX, pairs)  44.7 us
    ppermute x8, starting transfers between devices, shift(): return lax.ppermute(x, CTX, pairs)  32.4 us
    all_gather x1, waiting for transfers between devices, shards(): lax.all_gather(normed_flat.reshape(nh, sub, width), 'y', axis=1)  24.9 us
    reduce_scatter x1, waiting for transfers between devices, shards(): out_sum = lax.psum_scatter(out_part, HEAD, scatter_dimension=0, tiled=True)  19.2 us
    all_gather x1, waiting for transfers between devices, shards(): og = lax.all_gather(og.reshape(ny * sub, cols), HEAD, axis=0, tiled=True)  13.3 us
    all_to_all x1, blocking collectives, shards(): lax.all_to_all(out_grad.reshape(sub, ny, cols).transpose(1, 0, 2), 'y', 0...  12.4 us
    all_to_all x1, waiting for transfers between devices, shards(): gn = lax.all_to_all(gn_part, 'y', 0, 0)  11.3 us
    all_to_all x1, waiting for transfers between devices, shards(): wg = lax.all_to_all(wg_sum.reshape(ny, rows, cols), 'y', 0, 0)  6.22 us
  transfers between devices with their start and end apart: 16, of which 13 were waited for; matrix products, arithmetic and copies ran while one was open for 11% of the time, Pallas kernels for 0%

profile of v1, /device:TPU:32, one launch (start us, length us, event | category | flops | bytes accessed | tf_op | source)
XLA Modules:
  0.0 246.0 jit_solution(1307441706818277080)
XLA Ops:
  9.4 12.4 %all_to_all.20 = bf16[4,32,1536]{2,1,0:T(8,128)(2,1)} all-to-all(bf16[4,32,1536]{2,1,0:T(8,128)(2,1)S(1)} %copy.96), channel_id=1, replica_groups=mesh['y'=4,'z'=8,'x'=4,'c'=2] {'y'}, dimensions={0} | all-to-all | bytes 786432 | tf_op jit(solution)/shard_map/all_to_all | solution.py:47
  24.8 3.8 %collective-permute-start = (bf16[528,128]{1,0:T(8,128)(2,1)S(1)}, bf16[528,128]{1,0:T(8,128)(2,1)S(1)}, u32[]{:S(2)}, u32[]{:S(2)}) collective-permute-start(bf16[528,128]{1,0:T(8,128)(2,1)S(1)} %concatenate.24), channel_id=1, source_target_pairs={{0,8},{8,16},{16,24},{24,32},{32,40},{40,48},{48,56},{56,64},{64,7... | collective-permute-start | bytes 405512 | tf_op jit(solution)/shard_map/ppermute | solution.py:18
  29.5 4.4 %collective-permute-done = bf16[528,128]{1,0:T(8,128)(2,1)S(1)} collective-permute-done((bf16[528,128]{1,0:T(8,128)(2,1)S(1)}, bf16[528,128]{1,0:T(8,128)(2,1)S(1)}, u32[]{:S(2)}, u32[]{:S(2)}) %collective-permute-start) | collective-permute-done | bytes 135200 | tf_op jit(solution)/shard_map/ppermute | solution.py:18
  35.7 2.9 %collective-permute-start.1 = (bf16[528,128]{1,0:T(8,128)(2,1)S(1)}, bf16[528,128]{1,0:T(8,128)(2,1)S(1)}, u32[]{:S(2)}, u32[]{:S(2)}) collective-permute-start(bf16[528,128]{1,0:T(8,128)(2,1)S(1)} %concatenate.25), channel_id=1, source_target_pairs={{0,8},{8,16},{16,24},{24,32},{32,40},{40,48},{48,56},{56,64},{64,7... | collective-permute-start | bytes 405512 | tf_op jit(solution)/shard_map/ppermute | solution.py:18
  38.7 5.8 %collective-permute-done.1 = bf16[528,128]{1,0:T(8,128)(2,1)S(1)} collective-permute-done((bf16[528,128]{1,0:T(8,128)(2,1)S(1)}, bf16[528,128]{1,0:T(8,128)(2,1)S(1)}, u32[]{:S(2)}, u32[]{:S(2)}) %collective-permute-start.1) | collective-permute-done | bytes 135200 | tf_op jit(solution)/shard_map/ppermute | solution.py:18
  46.4 7.4 %collective-permute-start.2 = (bf16[528,128]{1,0:T(8,128)(2,1)S(1)}, bf16[528,128]{1,0:T(8,128)(2,1)S(1)}, u32[]{:S(2)}, u32[]{:S(2)}) collective-permute-start(bf16[528,128]{1,0:T(8,128)(2,1)S(1)} %concatenate.26), channel_id=1, source_target_pairs={{0,16},{8,24},{16,32},{24,40},{32,48},{40,56},{48,64},{56,72},{64,... | collective-permute-start | bytes 405512 | tf_op jit(solution)/shard_map/ppermute | solution.py:18
  54.2 3.2 %collective-permute-done.2 = bf16[528,128]{1,0:T(8,128)(2,1)S(1)} collective-permute-done((bf16[528,128]{1,0:T(8,128)(2,1)S(1)}, bf16[528,128]{1,0:T(8,128)(2,1)S(1)}, u32[]{:S(2)}, u32[]{:S(2)}) %collective-permute-start.2) | collective-permute-done | bytes 135200 | tf_op jit(solution)/shard_map/ppermute | solution.py:18
  60.0 11.0 %collective-permute-start.3 = (bf16[528,128]{1,0:T(8,128)(2,1)}, bf16[528,128]{1,0:T(8,128)(2,1)}, u32[]{:S(2)}, u32[]{:S(2)}) collective-permute-start(bf16[528,128]{1,0:T(8,128)(2,1)} %concatenate.27), channel_id=1, source_target_pairs={{0,32},{8,40},{16,48},{24,56},{32,64},{40,72},{48,80},{56,88},{64,... | collective-permute-start | bytes 405512 | tf_op jit(solution)/shard_map/ppermute | solution.py:18
  71.0 13.3 %all-gather.8.cloned.1.call-done = bf16[1024,1536]{1,0:T(8,128)(2,1)} async-done(((bf16[128,1536]{1,0:T(8,128)(2,1)}), bf16[1024,1536]{1,0:T(8,128)(2,1)}) %all-gather.8.cloned.1.call-update) | async-done | bytes 3145744 | tf_op jit(solution)/shard_map/all_gather | solution.py:48
  84.3 4.1 %convolution_convert_fusion.2 = bf16[1024,512]{1,0:T(8,128)(2,1)S(1)} fusion(bf16[1024,1536]{1,0:T(8,128)(2,1)} %all-gather.8.cloned.1.call-done, bf16[1536,512]{1,0:T(8,128)(2,1)} %all-gather.6.cloned.1.call-done), kind=kOutput, calls=%fused_computation.3 | convolution fusion | flops 1611137024 | bytes 5767168 | tf_op jit(solution)/shard_map/dot_general | solution.py:76
  89.5 4.4 %all-to-all-start.2 = ((bf16[4,8,32,512]{3,2,1,0:T(8,128)(2,1)}), bf16[4,8,32,512]{3,2,1,0:T(8,128)(2,1)S(1)}, u32[]{:S(2)}, u32[]{:S(2)}) async-start(bf16[4,8,32,512]{3,2,1,0:T(8,128)(2,1)} %bitcast.118), calls=%async_computation.3 | async-start | bytes 2097152 | tf_op jit(solution)/shard_map/all_to_all | solution.py:78
  98.1 11.3 %all-to-all-done.2 = bf16[4,8,32,512]{3,2,1,0:T(8,128)(2,1)S(1)} async-done(((bf16[4,8,32,512]{3,2,1,0:T(8,128)(2,1)}), bf16[4,8,32,512]{3,2,1,0:T(8,128)(2,1)S(1)}, u32[]{:S(2)}, u32[]{:S(2)}) %all-to-all-start.2) | async-done | bytes 1048608 | tf_op jit(solution)/shard_map/all_to_all | solution.py:78
  111.3 24.9 %all-gather.4.cloned.1.call-done = bf16[8,4,32,512]{3,2,0,1:T(8,128)(2,1)} async-done(((bf16[8,1,32,512]{3,2,0,1:T(8,128)(2,1)}), bf16[8,4,32,512]{3,2,0,1:T(8,128)(2,1)}) %all-gather.4.cloned.1.call-update) | async-done | bytes 1048592 | tf_op jit(solution)/shard_map/all_gather | solution.py:81
  137.5 3.7 %convolution_convert_fusion.1 = bf16[512,1536]{1,0:T(8,128)(2,1)S(1)} fusion(bf16[1024,512]{1,0:T(8,128)(2,1)S(1)} %bitcast.134, bf16[1024,1536]{1,0:T(8,128)(2,1)} %all-gather.8.cloned.1.call-done), kind=kOutput, calls=%fused_computation.1 | convolution fusion | flops 1611399168 | bytes 5767168 | tf_op jit(solution)/shard_map/dot_general | solution.py:90
  142.6 4.9 %convolution_convert_fusion = bf16[1024,1536]{1,0:T(8,128)(2,1)} fusion(bf16[1024,512]{1,0:T(8,128)(2,1)S(1)} %bitcast.135, bf16[1536,512]{1,0:T(8,128)(2,1)} %all-gather.6.cloned.1.call-done), kind=kOutput, calls=%fused_computation | convolution fusion | flops 1612185600 | bytes 5767168 | tf_op jit(solution)/shard_map/dot_general | solution.py:83
  150.8 3.9 %collective-permute-done.4 = bf16[528,128]{1,0:T(8,128)(2,1)S(1)} collective-permute-done((bf16[528,128]{1,0:T(8,128)(2,1)S(1)}, bf16[528,128]{1,0:T(8,128)(2,1)S(1)}, u32[]{:S(2)}, u32[]{:S(2)}) %collective-permute-start.4) | collective-permute-done | bytes 135200 | tf_op jit(solution)/shard_map/ppermute | solution.py:18
  160.0 4.1 %collective-permute-done.5 = bf16[528,128]{1,0:T(8,128)(2,1)S(1)} collective-permute-done((bf16[528,128]{1,0:T(8,128)(2,1)S(1)}, bf16[528,128]{1,0:T(8,128)(2,1)S(1)}, u32[]{:S(2)}, u32[]{:S(2)}) %collective-permute-start.5) | collective-permute-done | bytes 135200 | tf_op jit(solution)/shard_map/ppermute | solution.py:18
  167.5 14.1 %collective-permute-done.6 = bf16[528,128]{1,0:T(8,128)(2,1)S(1)} collective-permute-done((bf16[528,128]{1,0:T(8,128)(2,1)S(1)}, bf16[528,128]{1,0:T(8,128)(2,1)S(1)}, u32[]{:S(2)}, u32[]{:S(2)}) %collective-permute-start.6) | collective-permute-done | bytes 135200 | tf_op jit(solution)/shard_map/ppermute | solution.py:18
  185.0 9.3 %collective-permute-done.7 = bf16[528,128]{1,0:T(8,128)(2,1)S(1)} collective-permute-done((bf16[528,128]{1,0:T(8,128)(2,1)S(1)}, bf16[528,128]{1,0:T(8,128)(2,1)S(1)}, u32[]{:S(2)}, u32[]{:S(2)}) %collective-permute-start.7) | collective-permute-done | bytes 135200 | tf_op jit(solution)/shard_map/ppermute | solution.py:18
  196.2 5.6 %all-to-all-start.3 = ((bf16[4,16,1536]{2,1,0:T(8,128)(2,1)}), bf16[4,16,1536]{2,1,0:T(8,128)(2,1)S(1)}, u32[]{:S(2)}, u32[]{:S(2)}) async-start(bf16[4,16,1536]{2,1,0:T(8,128)(2,1)} %bitcast.144), calls=%async_computation.5 | async-start | bytes 393216 | tf_op jit(solution)/shard_map/all_to_all | solution.py:96
  201.8 6.2 %all-to-all-done.3 = bf16[4,16,1536]{2,1,0:T(8,128)(2,1)S(1)} async-done(((bf16[4,16,1536]{2,1,0:T(8,128)(2,1)}), bf16[4,16,1536]{2,1,0:T(8,128)(2,1)S(1)}, u32[]{:S(2)}, u32[]{:S(2)}) %all-to-all-start.3) | async-done | bytes 196640 | tf_op jit(solution)/shard_map/all_to_all | solution.py:96
  208.1 19.2 %reduce-scatter.3.cloned.1.call-done = bf16[128,1536]{1,0:T(8,128)(2,1)} async-done(((bf16[1024,1536]{1,0:T(8,128)(2,1)}), bf16[128,1536]{1,0:T(8,128)(2,1)}) %reduce-scatter.3.cloned.1.call-update) | async-done | bytes 393232 | tf_op jit(solution)/shard_map/reduce_scatter | solution.py:86
  227.2 4.1 %all-to-all-start = ((bf16[4,32,1536]{2,1,0:T(8,128)(2,1)}), bf16[4,32,1536]{2,1,0:T(8,128)(2,1)S(1)}, u32[]{:S(2)}, u32[]{:S(2)}) async-start(bf16[4,32,1536]{2,1,0:T(8,128)(2,1)} %bitcast.141), calls=%async_computation.1 | async-start | bytes 786432 | tf_op jit(solution)/shard_map/all_to_all | solution.py:87
  234.2 4.5 %all-to-all-done = bf16[4,32,1536]{2,1,0:T(8,128)(2,1)S(1)} async-done(((bf16[4,32,1536]{2,1,0:T(8,128)(2,1)}), bf16[4,32,1536]{2,1,0:T(8,128)(2,1)S(1)}, u32[]{:S(2)}, u32[]{:S(2)}) %all-to-all-start) | async-done | bytes 393248 | tf_op jit(solution)/shard_map/all_to_all | solution.py:87
  (96 shorter events, 31.7 us)
Async XLA Ops:
  7.2 17.4 %copy-start = (bf16[256,512]{1,0:T(8,128)(2,1)S(1)}, bf16[256,512]{1,0:T(8,128)(2,1)}, u32[]{:S(2)}) copy-start(bf16[256,512]{1,0:T(8,128)(2,1)} %param.8) | copy-start | bytes 786436
  7.2 14.7 %copy-start.8 = (s32[256]{0:T(256)S(1)}, s32[256]{0:T(256)}, u32[]{:S(2)}) copy-start(s32[256]{0:T(256)} %param.9) | copy-start | bytes 3076
  7.2 14.7 %copy-start.1 = (bf16[256,512]{1,0:T(8,128)(2,1)S(1)}, bf16[256,512]{1,0:T(8,128)(2,1)}, u32[]{:S(2)}) copy-start(bf16[256,512]{1,0:T(8,128)(2,1)} %param.7) | copy-start | bytes 786436
  7.2 63.8 %all-gather.6.cloned.1.call-start = ((), (), s32[]{:S(2)}) async-start(), calls=%async_computation.7 | async-start | bytes 1769472 | tf_op jit(solution)/shard_map/all_gather | solution.py:46
  7.9 21.4 %copy-start.5 = (bf16[256,512]{1,0:T(8,128)(2,1)S(1)}, bf16[256,512]{1,0:T(8,128)(2,1)}, u32[]{:S(2)}) copy-start(bf16[256,512]{1,0:T(8,128)(2,1)} %param.6) | copy-start | bytes 786436
  7.9 76.3 %all-gather.8.cloned.1.call-start = ((), (), s32[]{:S(2)}) async-start(), calls=%async_computation.9 | async-start | bytes 3538944 | tf_op jit(solution)/shard_map/all_gather | solution.py:48
  24.8 9.0 %collective-permute-start = (bf16[528,128]{1,0:T(8,128)(2,1)S(1)}, bf16[528,128]{1,0:T(8,128)(2,1)S(1)}, u32[]{:S(2)}, u32[]{:S(2)}) collective-permute-start(bf16[528,128]{1,0:T(8,128)(2,1)S(1)} %concatenate.24), channel_id=1, source_target_pairs={{0,8},{8,16},{16,24},{24,32},{32,40},{40,48},{48,56},{56,64},{64,7... | collective-permute-start | bytes 405512 | tf_op jit(solution)/shard_map/ppermute | solution.py:18
  35.7 8.8 %collective-permute-start.1 = (bf16[528,128]{1,0:T(8,128)(2,1)S(1)}, bf16[528,128]{1,0:T(8,128)(2,1)S(1)}, u32[]{:S(2)}, u32[]{:S(2)}) collective-permute-start(bf16[528,128]{1,0:T(8,128)(2,1)S(1)} %concatenate.25), channel_id=1, source_target_pairs={{0,8},{8,16},{16,24},{24,32},{32,40},{40,48},{48,56},{56,64},{64,7... | collective-permute-start | bytes 405512 | tf_op jit(solution)/shard_map/ppermute | solution.py:18
  38.7 19.9 %copy-start.6 = (pred[256,256]{1,0:T(8,128)(4,1)}, pred[256,256]{1,0:T(8,128)(4,1)S(1)}, u32[]{:S(2)}) copy-start(pred[256,256]{1,0:T(8,128)(4,1)S(1)} %fusion.22) | copy-start | bytes 196612
  46.4 10.9 %collective-permute-start.2 = (bf16[528,128]{1,0:T(8,128)(2,1)S(1)}, bf16[528,128]{1,0:T(8,128)(2,1)S(1)}, u32[]{:S(2)}, u32[]{:S(2)}) collective-permute-start(bf16[528,128]{1,0:T(8,128)(2,1)S(1)} %concatenate.26), channel_id=1, source_target_pairs={{0,16},{8,24},{16,32},{24,40},{32,48},{40,56},{48,64},{56,72},{64,... | collective-permute-start | bytes 405512 | tf_op jit(solution)/shard_map/ppermute | solution.py:18
  57.4 31.0 %copy-start.3 = (bf16[528,128]{1,0:T(8,128)(2,1)}, bf16[528,128]{1,0:T(8,128)(2,1)S(1)}, u32[]{:S(2)}) copy-start(bf16[528,128]{1,0:T(8,128)(2,1)S(1)} %collective-permute-done.2) | copy-start | bytes 405508
  60.0 34.3 %collective-permute-start.3 = (bf16[528,128]{1,0:T(8,128)(2,1)}, bf16[528,128]{1,0:T(8,128)(2,1)}, u32[]{:S(2)}, u32[]{:S(2)}) collective-permute-start(bf16[528,128]{1,0:T(8,128)(2,1)} %concatenate.27), channel_id=1, source_target_pairs={{0,32},{8,40},{16,48},{24,56},{32,64},{40,72},{48,80},{56,88},{64,... | collective-permute-start | bytes 405512 | tf_op jit(solution)/shard_map/ppermute | solution.py:18
  89.5 7.3 %copy-start.4 = (bf16[528,128]{1,0:T(8,128)(2,1)S(1)}, bf16[528,128]{1,0:T(8,128)(2,1)}, u32[]{:S(2)}) copy-start(bf16[528,128]{1,0:T(8,128)(2,1)} %copy-done.3) | copy-start | bytes 405508
  89.5 19.9 %all-to-all-start.2 = ((bf16[4,8,32,512]{3,2,1,0:T(8,128)(2,1)}), bf16[4,8,32,512]{3,2,1,0:T(8,128)(2,1)S(1)}, u32[]{:S(2)}, u32[]{:S(2)}) async-start(bf16[4,8,32,512]{3,2,1,0:T(8,128)(2,1)} %bitcast.118), calls=%async_computation.3 | async-start | bytes 2097152 | tf_op jit(solution)/shard_map/all_to_all | solution.py:78
  93.9 42.2 %all-gather.4.cloned.1.call-start = ((), (), s32[]{:S(2)}) async-start(), calls=%async_computation.6 | async-start | bytes 1310720 | tf_op jit(solution)/shard_map/all_gather | solution.py:81
  111.3 84.9 %reduce-scatter.5.cloned.1.call-start = ((), (), s32[]{:S(2)}) async-start(), calls=%async_computation.10 | async-start | bytes 1769472 | tf_op jit(solution)/shard_map/reduce_scatter | solution.py:95
  142.6 84.7 %reduce-scatter.3.cloned.1.call-start = ((), (), s32[]{:S(2)}) async-start(), calls=%async_computation.8 | async-start | bytes 3538944 | tf_op jit(solution)/shard_map/reduce_scatter | solution.py:86
  147.8 6.9 %collective-permute-start.4 = (bf16[528,128]{1,0:T(8,128)(2,1)S(1)}, bf16[528,128]{1,0:T(8,128)(2,1)S(1)}, u32[]{:S(2)}, u32[]{:S(2)}) collective-permute-start(bf16[528,128]{1,0:T(8,128)(2,1)S(1)} %concatenate.28), channel_id=1, source_target_pairs={{8,0},{16,8},{24,16},{32,24},{40,32},{48,40},{56,48},{64,56},{72,6... | collective-permute-start | bytes 405512 | tf_op jit(solution)/shard_map/ppermute | solution.py:18
  156.5 7.5 %collective-permute-start.5 = (bf16[528,128]{1,0:T(8,128)(2,1)S(1)}, bf16[528,128]{1,0:T(8,128)(2,1)S(1)}, u32[]{:S(2)}, u32[]{:S(2)}) collective-permute-start(bf16[528,128]{1,0:T(8,128)(2,1)S(1)} %concatenate.29), channel_id=1, source_target_pairs={{8,0},{16,8},{24,16},{32,24},{40,32},{48,40},{56,48},{64,56},{72,6... | collective-permute-start | bytes 405512 | tf_op jit(solution)/shard_map/ppermute | solution.py:18
  166.0 15.6 %collective-permute-start.6 = (bf16[528,128]{1,0:T(8,128)(2,1)S(1)}, bf16[528,128]{1,0:T(8,128)(2,1)S(1)}, u32[]{:S(2)}, u32[]{:S(2)}) collective-permute-start(bf16[528,128]{1,0:T(8,128)(2,1)S(1)} %concatenate.30), channel_id=1, source_target_pairs={{16,0},{24,8},{32,16},{40,24},{48,32},{56,40},{64,48},{72,56},{80,... | collective-permute-start | bytes 405512 | tf_op jit(solution)/shard_map/ppermute | solution.py:18
  167.5 63.8 %copy-start.2 = (bf16[256,512]{1,0:T(8,128)(2,1)S(1)}, bf16[256,512]{1,0:T(8,128)(2,1)}, u32[]{:S(2)}) copy-start(bf16[256,512]{1,0:T(8,128)(2,1)} %param.7) | copy-start | bytes 786436
  183.5 10.8 %collective-permute-start.7 = (bf16[528,128]{1,0:T(8,128)(2,1)S(1)}, bf16[528,128]{1,0:T(8,128)(2,1)S(1)}, u32[]{:S(2)}, u32[]{:S(2)}) collective-permute-start(bf16[528,128]{1,0:T(8,128)(2,1)S(1)} %concatenate.31), channel_id=1, source_target_pairs={{32,0},{40,8},{48,16},{56,24},{64,32},{72,40},{80,48},{88,56},{96,... | collective-permute-start | bytes 405512 | tf_op jit(solution)/shard_map/ppermute | solution.py:18
  196.2 11.9 %all-to-all-start.3 = ((bf16[4,16,1536]{2,1,0:T(8,128)(2,1)}), bf16[4,16,1536]{2,1,0:T(8,128)(2,1)S(1)}, u32[]{:S(2)}, u32[]{:S(2)}) async-start(bf16[4,16,1536]{2,1,0:T(8,128)(2,1)} %bitcast.144), calls=%async_computation.5 | async-start | bytes 393216 | tf_op jit(solution)/shard_map/all_to_all | solution.py:96
  227.2 11.5 %all-to-all-start = ((bf16[4,32,1536]{2,1,0:T(8,128)(2,1)}), bf16[4,32,1536]{2,1,0:T(8,128)(2,1)S(1)}, u32[]{:S(2)}, u32[]{:S(2)}) async-start(bf16[4,32,1536]{2,1,0:T(8,128)(2,1)} %bitcast.141), calls=%async_computation.1 | async-start | bytes 786432 | tf_op jit(solution)/shard_map/all_to_all | solution.py:87
  (1 other events, 2.7 us)
Sparse Core Ops, SparseCore 0:
  9.8 43.2 all-gather.5
  55.0 29.2 all-gather.7
  111.4 24.7 all-gather.3
  142.7 43.1 reduce-scatter.4
  188.3 38.8 reduce-scatter.2

commit v2 on v1

v2 whole, which is shorter than its diff:
```python
import jax
import jax.numpy as jnp
from jax import lax
from jax.sharding import Mesh, PartitionSpec as P

HD = 128
EPSILON = 1e-05
BF = jnp.bfloat16
F32 = jnp.float32
CTX = ("y", "z")
HEAD = ("x", "c")
SWAP = [(0, 1), (1, 0)]


def turn(x, axis, by):
    count = lax.axis_size(axis)
    return lax.ppermute(x, axis, [(i, (i + by) % count) for i in range(count)])


def row_state(local, first_marks, last_marks, marks, backward, beside=()):
    nz, ny = lax.axis_size("z"), lax.axis_size("y")
    rows = local.shape[0] // nz
    slices = local.astype(BF).reshape(nz, rows, HD)
    if marks is not None:
        slices = jnp.concatenate(
            [slices, jnp.broadcast_to(marks[None], (nz,) + marks.shape)], axis=1
        )
    got = lax.all_to_all(slices, "z", 0, 0)
    if marks is not None:
        first_marks = got[:, rows, 0].astype(F32)
        last_marks = got[:, rows + 8, 0].astype(F32)
    states = got[:, :rows].astype(F32)
    place = jnp.arange(nz)
    if backward:
        takes = (first_marks[None, :] == last_marks[:, None]) & (place[None, :] > place[:, None])
        edge, enters, sends = first_marks[0], last_marks, first_marks
        pairs = [(i, i - 1) for i in range(1, ny)]
    else:
        takes = (last_marks[None, :] == first_marks[:, None]) & (place[None, :] < place[:, None])
        edge, enters, sends = last_marks[nz - 1], first_marks, last_marks
        pairs = [(i, i + 1) for i in range(ny - 1)]
    carry = jnp.sum(jnp.where((sends == edge)[:, None, None], states, 0.0), axis=0)
    message = jnp.concatenate([carry.astype(BF), jnp.zeros((16, HD), BF) + edge.astype(BF)])
    message = lax.ppermute(message, "y", pairs)
    inside = jnp.sum(jnp.where(takes[:, :, None, None], states[None], 0.0), axis=1)
    linked = (message[rows, 0].astype(F32) == enters)[:, None, None]
    total = inside + jnp.where(linked, message[None, :rows].astype(F32), 0.0)
    total, beside = lax.optimization_barrier((total.astype(BF), beside))
    out = lax.all_to_all(total, "z", 0, 0)
    return out.reshape(local.shape), first_marks, last_marks, beside


def shards(queries, key_rows, value_rows, doc_ids, out_grad, out_weight):
    tok, width = queries.shape
    heads = width // HD
    ny, nz, nx = lax.axis_size("y"), lax.axis_size("z"), lax.axis_size("x")
    cols = out_grad.shape[1] // ny
    sub = out_grad.shape[0]
    half = nx * ny * sub
    core = lax.axis_index("c")

    query_heads = queries.reshape(tok, heads, HD)
    key_heads = key_rows.reshape(tok, heads, HD)
    value_heads = value_rows.reshape(tok, heads, HD)
    docs = doc_ids.astype(F32)
    first_doc, last_doc = docs[0], docs[-1]
    causal = jnp.tril(jnp.ones((tok, tok), dtype=bool))
    allowed = (causal & (doc_ids[:, None] == doc_ids[None, :]))[None]
    in_first = (docs == first_doc)[:, None, None]
    in_last = (docs == last_doc)[:, None, None]

    weight_t = lax.all_gather(out_weight.T, "z", axis=0, tiled=True)
    pieces = out_grad.reshape(sub, ny, cols).transpose(1, 0, 2)
    row, place = lax.axis_index("y"), lax.axis_index("x")
    piece = [lax.dynamic_index_in_dim(pieces, row, 0, False)]
    for step in range(1, ny):
        sent = lax.dynamic_index_in_dim(pieces, (row - step) % ny, 0, False)
        piece.append(turn(sent, "y", -step))
    piece = jnp.stack(piece)

    key_last = jnp.where(in_last, key_heads, jnp.zeros_like(key_heads))
    local_state = jnp.einsum("thd,the->hde", key_last, value_heads, preferred_element_type=F32)
    ones = jnp.ones((8, HD), F32)
    marks = jnp.concatenate([ones * (first_doc + 1.0), ones * (last_doc + 1.0)]).astype(BF)
    og_own = [piece] + [turn(piece, "x", -step) for step in range(1, nx)]
    prior, first_marks, last_marks, og_own = row_state(
        local_state.reshape(heads * HD, HD), None, None, marks, False, og_own
    )
    og_own = jnp.stack(og_own).reshape(half, cols)
    og_other = lax.ppermute(og_own, "c", SWAP)
    prior = prior.reshape(heads, HD, HD)

    scores = jnp.einsum("thd,shd->hts", query_heads, key_heads, preferred_element_type=F32)
    weights = jnp.where(allowed, scores, F32(0.0)).astype(BF)
    inter = jnp.einsum("thd,hde->the", query_heads, prior, preferred_element_type=F32)
    mixed = jnp.einsum(
        "hts,she->the", weights, value_heads, preferred_element_type=F32
    ) + jnp.where(in_first, inter, F32(0.0))
    inv_norm = lax.rsqrt(jnp.mean(mixed * mixed, axis=-1, keepdims=True) + EPSILON)
    normed = mixed * inv_norm

    by_core = normed.astype(BF).reshape(nx, 2, sub, width).transpose(1, 0, 2, 3)
    by_core = jnp.where(core == 0, by_core, by_core[::-1])
    by_core = jnp.concatenate([by_core, by_core], axis=1)
    by_core = lax.dynamic_slice_in_dim(by_core, place, nx, 1)
    gn_part = jnp.stack(
        [jnp.dot(g, weight_t, preferred_element_type=F32).astype(BF) for g in (og_own, og_other)]
    )
    gn_part = gn_part.reshape(2, nx, ny, sub, width).transpose(2, 0, 1, 3, 4)
    normed_all = [by_core] + [turn(by_core, "y", -step) for step in range(1, ny)]
    normed_all = jnp.stack(normed_all, axis=2).reshape(2, half, width)
    gn_part, normed_all = lax.optimization_barrier((gn_part, normed_all))

    gn = gn_part[0].astype(F32)
    for step in range(1, ny):
        gn = gn + turn(gn_part[step], "y", step).astype(F32)
    gn = lax.dynamic_slice_in_dim(jnp.concatenate([gn, gn], axis=1), (nx - place) % nx, nx, 1)
    gn = jnp.where(core == 0, gn, gn[::-1])
    grad_normed = gn.transpose(1, 0, 2, 3).reshape(tok, heads, HD)

    def project(rows):
        return lax.dot_general(
            rows, weight_t, (((1,), (1,)), ((), ())), preferred_element_type=F32
        )

    wg_part = lax.dot_general(
        normed_all[0], og_own, (((0,), (0,)), ((), ())), preferred_element_type=F32
    ) + lax.dot_general(
        normed_all[1], og_other, (((0,), (0,)), ((), ())), preferred_element_type=F32
    )
    rows = width // (ny * nz)
    wg_part = wg_part.astype(BF).reshape(ny, nz, rows, cols).transpose(1, 0, 2, 3)
    wg_sum = lax.psum_scatter(wg_part.reshape(width, cols), "z", scatter_dimension=0, tiled=True)
    out_sent = lax.ppermute(project(normed_all[1]).astype(BF), "c", SWAP)
    out_own = (project(normed_all[0]) + out_sent.astype(F32)).astype(BF)
    out_own = out_own.reshape(nx, ny * sub, cols)
    out_sum = out_own[0].astype(F32)
    for step in range(1, nx):
        out_sum = out_sum + turn(out_own[step], "x", step).astype(F32)
    out_sum = out_sum.astype(BF).reshape(ny, sub, cols)
    out_sum = jnp.concatenate([out_sum, out_sum])
    out_sum = lax.dynamic_slice_in_dim(out_sum, (ny - row) % ny, ny, 0)
    last = jnp.concatenate(
        [out_sum, wg_sum.reshape(ny, rows, cols)], axis=1
    )
    last = lax.all_to_all(last, "y", 0, 0).transpose(1, 0, 2).reshape(sub + rows, ny * cols)
    layer_out, weight_grad = last[:sub], last[sub:]

    mixed_grad = (
        inv_norm * (grad_normed - normed * jnp.mean(grad_normed * normed, axis=-1, keepdims=True))
    ).astype(BF)
    query_first = jnp.where(in_first, query_heads, jnp.zeros_like(query_heads))
    local_future = jnp.einsum("thd,the->hde", query_first, mixed_grad, preferred_element_type=F32)
    future, unused, unused, unused = row_state(
        local_future.reshape(heads * HD, HD), first_marks, last_marks, None, True
    )
    future = future.reshape(heads, HD, HD)

    grad_raw = jnp.einsum("the,she->hts", mixed_grad, value_heads, preferred_element_type=F32)
    grad_scores = jnp.where(allowed, grad_raw, F32(0.0)).astype(BF)
    query_grad = jnp.einsum(
        "hts,shd->thd", grad_scores, key_heads, preferred_element_type=F32
    ) + jnp.where(
        in_first,
        jnp.einsum("the,hde->thd", mixed_grad, prior, preferred_element_type=F32),
        F32(0.0),
    )
    key_grad = jnp.einsum(
        "hts,thd->shd", grad_scores, query_heads, preferred_element_type=F32
    ) + jnp.where(
        in_last,
        jnp.einsum("she,hde->shd", value_heads, future, preferred_element_type=F32),
        F32(0.0),
    )
    value_grad = jnp.einsum(
        "hts,the->she", weights, mixed_grad, preferred_element_type=F32
    ) + jnp.where(
        in_last,
        jnp.einsum("shd,hde->she", key_heads, future, preferred_element_type=F32),
        F32(0.0),
    )
    return (
        layer_out,
        query_grad.astype(BF).reshape(tok, width),
        key_grad.astype(BF).reshape(tok, width),
        value_grad.astype(BF).reshape(tok, width),
        weight_grad,
    )


def solution(mesh):
    grid = Mesh(mesh.devices.reshape(4, 8, 4, 2), ("y", "z", "x", "c"))
    return jax.shard_map(
        shards,
        mesh=grid,
        in_specs=(
            P(CTX, HEAD),
            P(CTX, HEAD),
            P(CTX, HEAD),
            P(CTX),
            P(CTX + HEAD, None),
            P(HEAD, CTX),
        ),
        out_specs=(
            P(CTX + HEAD, None),
            P(CTX, HEAD),
            P(CTX, HEAD),
            P(CTX, HEAD),
            P(HEAD + CTX, None),
        ),
        check_vma=False,
    )
```

time: 247 us -> 179 us (0.72)
  waiting for transfers between devices: 125 us -> 48.8 us
  other arithmetic: 3.25 us -> 18.1 us
  blocking collectives: 12.4 us -> 0 us
  starting transfers between devices: 46.6 us -> 57.4 us
  between operations: 26 us -> 18.6 us
  matrix products: 15.9 us -> 19.5 us
    all_gather x2 -> x0, waiting for transfers between devices: 38.1 us -> none  [the longest x1 24.9 us: shards(): lax.all_gather(normed_flat.reshape(nh, sub, width), 'y', axis=1)]
    reduce_scatter x2 -> x1, waiting for transfers between devices: 19.2 us -> 0.02 us  [shards(): lax.psum_scatter(wg_part.reshape(width, cols), 'z', scatter_dimension=0,...]
    all_to_all x3 -> x5, starting transfers between devices: 14.1 us -> 31.9 us  [the longest x2 14.4 us: row_state(): got = lax.all_to_all(slices, 'z', 0, 0)]
    ppermute x8 -> x19, waiting for transfers between devices: 44.7 us -> 28.7 us  [the longest x15 28.3 us: turn(): return lax.ppermute(x, axis, [(i, (i + by) % count) for i in range(count)])]
    all_to_all x1 -> x0, blocking collectives: 12.4 us -> none  [shards(): lax.all_to_all(out_grad.reshape(sub, ny, cols).transpose(1, 0, 2), 'y', 0...]
    ppermute x8 -> x19, starting transfers between devices: 32.4 us -> 25.5 us  [the longest x15 22.8 us: turn(): return lax.ppermute(x, axis, [(i, (i + by) % count) for i in range(count)])]
    reshape x7 -> x5, local copies, waits for them, and re-layouts: 5.62 us -> 2.06 us  [the longest x1 1.28 us: shards(): wg_part.astype(BF).reshape(ny, nz, rows, cols).transpose(1, 0, 2, 3)]
    eq x0 -> x3, other arithmetic: none -> 3.24 us  [the longest x2 2.28 us: row_state(): sends == edge]
  transfers between devices with their start and end apart: 16 -> 26, of which waited for: 13 -> 15; matrix products, arithmetic and copies ran while one was open for 11% -> 26% of each run, Pallas kernels for 0% -> 0%
where the time goes in v2:
time: 179 us; the launch traced here: 178 us
  starting transfers between devices  57.4 us (32%)
  waiting for transfers between devices  48.8 us (27%)
  matrix products  19.5 us (11%)
  between operations  18.6 us (10%)
  other arithmetic  18.1 us (10%)
  local copies, waits for them, and re-layouts  15.6 us (9%)
    ppermute x15, waiting for transfers between devices, turn(): return lax.ppermute(x, axis, [(i, (i + by) % count) for i in range(count)])  28.3 us
    ppermute x15, starting transfers between devices, turn(): return lax.ppermute(x, axis, [(i, (i + by) % count) for i in range(count)])  22.8 us
    all_to_all x2, starting transfers between devices, row_state(): got = lax.all_to_all(slices, 'z', 0, 0)  14.4 us
    all_to_all x2, starting transfers between devices, row_state(): out = lax.all_to_all(total, 'z', 0, 0)  10.8 us
    all_to_all x1, waiting for transfers between devices, shards(): lax.all_to_all(last, 'y', 0, 0).transpose(1, 0, 2)  6.74 us
    all_to_all x1, starting transfers between devices, shards(): lax.all_to_all(last, 'y', 0, 0).transpose(1, 0, 2)  6.73 us
    all_to_all x2, waiting for transfers between devices, row_state(): got = lax.all_to_all(slices, 'z', 0, 0)  6.55 us
    dot_general x2, matrix products, project(): lax.dot_general(rows, weight_t, (((1,), (1,)), ((), ())), preferred_eleme...  6.54 us
  transfers between devices with their start and end apart: 26, of which 15 were waited for; matrix products, arithmetic and copies ran while one was open for 26% of the time, Pallas kernels for 0%

profile of v2, /device:TPU:32, one launch (start us, length us, event | category | flops | bytes accessed | tf_op | source)
XLA Modules:
  0.0 178.1 jit_solution(14836420990286779253)
XLA Ops:
  14.7 8.6 %all-to-all-start = ((bf16[8,80,128]{2,1,0:T(8,128)(2,1)}), bf16[8,80,128]{2,1,0:T(8,128)(2,1)S(1)}, u32[]{:S(2)}, u32[]{:S(2)}) async-start(bf16[8,80,128]{2,1,0:T(8,128)(2,1)} %pad_maximum_fusion.5), calls=%async_computation | async-start | bytes 327680 | tf_op jit(solution)/shard_map/all_to_all | solution.py:28
  24.4 3.1 %collective-permute-start.1 = (bf16[32,1536]{1,0:T(8,128)(2,1)S(1)}, bf16[32,1536]{1,0:T(8,128)(2,1)S(1)}, u32[]{:S(2)}, u32[]{:S(2)}) collective-permute-start(bf16[32,1536]{1,0:T(8,128)(2,1)S(1)} %bitcast.208), channel_id=1, source_target_pairs={{0,192},{64,0},{128,64},{192,128},{1,193},{65,1},{129,65},{193,129... | collective-permute-start | bytes 294920 | tf_op jit(solution)/shard_map/ppermute | solution.py:17
  31.3 2.6 %collective-permute-done.2 = bf16[32,1536]{1,0:T(8,128)(2,1)S(1)} collective-permute-done((bf16[32,1536]{1,0:T(8,128)(2,1)S(1)}, bf16[32,1536]{1,0:T(8,128)(2,1)S(1)}, u32[]{:S(2)}, u32[]{:S(2)}) %collective-permute-start.2) | collective-permute-done | bytes 98336 | tf_op jit(solution)/shard_map/ppermute | solution.py:17
  36.5 2.7 %collective-permute-start.5 = (bf16[4,32,1536]{2,1,0:T(8,128)(2,1)S(1)}, bf16[4,32,1536]{2,1,0:T(8,128)(2,1)}, u32[]{:S(2)}, u32[]{:S(2)}) collective-permute-start(bf16[4,32,1536]{2,1,0:T(8,128)(2,1)S(1)} %pad_maximum_fusion.4), channel_id=1, source_target_pairs={{0,4},{2,6},{4,0},{6,2},{1,5},{3,7},{5,1},{7,3},{8,12},{10,14},{12... | collective-permute-start | bytes 1179656 | tf_op jit(solution)/shard_map/ppermute | solution.py:17
  49.0 5.9 %collective-permute-done.5 = bf16[4,32,1536]{2,1,0:T(8,128)(2,1)} collective-permute-done((bf16[4,32,1536]{2,1,0:T(8,128)(2,1)S(1)}, bf16[4,32,1536]{2,1,0:T(8,128)(2,1)}, u32[]{:S(2)}, u32[]{:S(2)}) %collective-permute-start.5) | collective-permute-done | bytes 393248 | tf_op jit(solution)/shard_map/ppermute | solution.py:17
  54.9 7.2 %all-to-all-start.1 = ((bf16[8,64,128]{2,1,0:T(8,128)(2,1)}), bf16[8,64,128]{2,1,0:T(8,128)(2,1)S(1)}, u32[]{:S(2)}, u32[]{:S(2)}) async-start(bf16[8,64,128]{2,1,0:T(8,128)(2,1)} %add_convert_fusion.3), calls=%async_computation.1 | async-start | bytes 262144 | tf_op jit(solution)/shard_map/all_to_all | solution.py:49
  63.6 6.1 %all-to-all-done.1 = bf16[8,64,128]{2,1,0:T(8,128)(2,1)S(1)} async-done(((bf16[8,64,128]{2,1,0:T(8,128)(2,1)}), bf16[8,64,128]{2,1,0:T(8,128)(2,1)S(1)}, u32[]{:S(2)}, u32[]{:S(2)}) %all-to-all-start.1) | async-done | bytes 131104 | tf_op jit(solution)/shard_map/all_to_all | solution.py:49
  74.7 4.0 %collective-permute-done.8 = bf16[2,4,32,512]{3,2,0,1:T(8,128)(2,1)S(1)} collective-permute-done((bf16[2,4,32,512]{3,2,0,1:T(8,128)(2,1)S(1)}, bf16[2,4,32,512]{3,2,0,1:T(8,128)(2,1)S(1)}, u32[]{:S(2)}, u32[]{:S(2)}) %collective-permute-start.8) | collective-permute-done | bytes 262176 | tf_op jit(solution)/shard_map/ppermute | solution.py:17
  78.7 2.1 %collective-permute-done.9 = bf16[2,4,32,512]{3,2,0,1:T(8,128)(2,1)} collective-permute-done((bf16[2,4,32,512]{3,2,0,1:T(8,128)(2,1)S(1)}, bf16[2,4,32,512]{3,2,0,1:T(8,128)(2,1)}, u32[]{:S(2)}, u32[]{:S(2)}) %collective-permute-start.9) | collective-permute-done | bytes 262176 | tf_op jit(solution)/shard_map/ppermute | solution.py:17
  80.8 2.7 %collective-permute-done.10 = bf16[2,4,32,512]{3,2,0,1:T(8,128)(2,1)} collective-permute-done((bf16[2,4,32,512]{3,2,0,1:T(8,128)(2,1)S(1)}, bf16[2,4,32,512]{3,2,0,1:T(8,128)(2,1)}, u32[]{:S(2)}, u32[]{:S(2)}) %collective-permute-start.10) | collective-permute-done | bytes 262176 | tf_op jit(solution)/shard_map/ppermute | solution.py:17
  85.7 2.5 %convolution_convert_fusion.2 = bf16[512,512]{1,0:T(8,128)(2,1)S(1)} fusion(bf16[512,1536]{1,0:T(8,128)(2,1)S(1)} %bitcast.171, bf16[1536,512]{1,0:T(8,128)(2,1)} %all-gather.2.cloned.1.call-done), kind=kOutput, calls=%fused_computation.10 | convolution fusion | flops 805568512 | bytes 3670016 | tf_op jit(solution)/shard_map/dot_general | solution.py:107
  88.2 2.4 %convolution_convert_fusion.1 = bf16[512,512]{1,0:T(8,128)(2,1)S(1)} fusion(bf16[512,1536]{1,0:T(8,128)(2,1)} %collective-permute-done.7, bf16[1536,512]{1,0:T(8,128)(2,1)S(1)} %copy-done.20), kind=kOutput, calls=%fused_computation.9 | convolution fusion | flops 805568512 | bytes 3670016 | tf_op jit(solution)/shard_map/dot_general | solution.py:107
  91.8 3.1 %collective-permute-start.17 = (bf16[2,4,32,512]{3,2,0,1:T(8,128)(2,1)}, bf16[2,4,32,512]{3,2,0,1:T(8,128)(2,1)}, u32[]{:S(2)}, u32[]{:S(2)}) collective-permute-start(bf16[2,4,32,512]{3,2,0,1:T(8,128)(2,1)} %get-tuple-element.47), channel_id=1, source_target_pairs={{0,192},{64,0},{128,64},{192,128},{1,193},{65,1},{129,65},{193,129... | collective-permute-start | bytes 786440 | tf_op jit(solution)/shard_map/ppermute | solution.py:17
  96.3 2.4 %fusion = bf16[512,1536]{1,0:T(8,128)(2,1)S(1)} fusion(f32[512,1536]{1,0:T(8,128)S(1)} %fusion.19, bf16[512,1536]{1,0:T(8,128)(2,1)} %collective-permute-done.7, bf16[2,512,512]{2,1,0:T(8,128)(2,1)S(1)} %bitcast.175), kind=kOutput, calls=%fused_computation.3 | convolution fusion | flops 806879232 | bytes 6815744 | tf_op jit(solution)/shard_map/dot_general | solution.py:128
  101.2 3.6 %convolution_convert_fusion = bf16[512,1536]{1,0:T(8,128)(2,1)} fusion(bf16[1536,512]{1,0:T(8,128)(2,1)} %all-gather.2.cloned.1.call-done, bf16[2,512,512]{2,1,0:T(8,128)(2,1)S(1)} %bitcast.176), kind=kOutput, calls=%fused_computation.2 | convolution fusion | flops 806092800 | bytes 3670016 | tf_op jit(solution)/shard_map/dot_general | solution.py:122
  108.6 5.8 %all-to-all-start.3 = ((bf16[8,64,128]{2,1,0:T(8,128)(2,1)}), bf16[8,64,128]{2,1,0:T(8,128)(2,1)S(1)}, u32[]{:S(2)}, u32[]{:S(2)}) async-start(bf16[8,64,128]{2,1,0:T(8,128)(2,1)} %bitcast.43), calls=%async_computation.4 | async-start | bytes 262144 | tf_op jit(solution)/shard_map/all_to_all | solution.py:28
  117.5 6.5 %all-to-all-done.3 = bf16[8,64,128]{2,1,0:T(8,128)(2,1)S(1)} async-done(((bf16[8,64,128]{2,1,0:T(8,128)(2,1)}), bf16[8,64,128]{2,1,0:T(8,128)(2,1)S(1)}, u32[]{:S(2)}, u32[]{:S(2)}) %all-to-all-start.3) | async-done | bytes 131104 | tf_op jit(solution)/shard_map/all_to_all | solution.py:28
  126.4 2.9 %add_convert_fusion = bf16[512,1536]{1,0:T(8,128)(2,1)S(1)} fusion(bf16[512,1536]{1,0:T(8,128)(2,1)} %collective-permute-done.11, bf16[1536,512]{1,0:T(8,128)(2,1)} %all-gather.2.cloned.1.call-done, bf16[2,512,512]{2,1,0:T(8,128)(2,1)S(1)} %bitcast.177), kind=kOutput, calls=%fused_computation.1 | convolution fusion | flops 807665664 | bytes 5242880 | tf_op jit(solution)/shard_map/dot_general | solution.py:122
  130.2 2.1 %collective-permute-start.12 = (bf16[128,1536]{1,0:T(8,128)(2,1)}, bf16[128,1536]{1,0:T(8,128)(2,1)}, u32[]{:S(2)}, u32[]{:S(2)}) collective-permute-start(bf16[128,1536]{1,0:T(8,128)(2,1)} %get-tuple-element.43), channel_id=1, source_target_pairs={{0,2},{2,4},{4,6},{6,0},{1,3},{3,5},{5,7},{7,1},{8,10},{10,12},{12... | collective-permute-start | bytes 1179656 | tf_op jit(solution)/shard_map/ppermute | solution.py:17
  138.3 3.6 %all-to-all-start.4 = ((bf16[8,64,128]{2,1,0:T(8,128)(2,1)}), bf16[8,64,128]{2,1,0:T(8,128)(2,1)S(1)}, u32[]{:S(2)}, u32[]{:S(2)}) async-start(bf16[8,64,128]{2,1,0:T(8,128)(2,1)} %add_convert_fusion.2), calls=%async_computation.5 | async-start | bytes 262144 | tf_op jit(solution)/shard_map/all_to_all | solution.py:49
  143.4 4.9 %collective-permute-done.14 = bf16[128,1536]{1,0:T(8,128)(2,1)} collective-permute-done((bf16[128,1536]{1,0:T(8,128)(2,1)S(1)}, bf16[128,1536]{1,0:T(8,128)(2,1)}, u32[]{:S(2)}, u32[]{:S(2)}) %collective-permute-start.14) | collective-permute-done | bytes 393248 | tf_op jit(solution)/shard_map/ppermute | solution.py:17
  148.4 2.2 %collective-permute-done.13 = bf16[128,1536]{1,0:T(8,128)(2,1)} collective-permute-done((bf16[128,1536]{1,0:T(8,128)(2,1)S(1)}, bf16[128,1536]{1,0:T(8,128)(2,1)}, u32[]{:S(2)}, u32[]{:S(2)}) %collective-permute-start.13) | collective-permute-done | bytes 393248 | tf_op jit(solution)/shard_map/ppermute | solution.py:17
  154.1 6.7 %all-to-all-start.2 = ((bf16[4,48,1536]{2,1,0:T(8,128)(2,1)}), bf16[4,48,1536]{2,1,0:T(8,128)(2,1)S(1)}, u32[]{:S(2)}, u32[]{:S(2)}) async-start(bf16[4,48,1536]{2,1,0:T(8,128)(2,1)} %pad_maximum_fusion.3), calls=%async_computation.3 | async-start | bytes 1179648 | tf_op jit(solution)/shard_map/all_to_all | solution.py:146
  163.0 6.7 %all-to-all-done.2 = bf16[4,48,1536]{2,1,0:T(8,128)(2,1)S(1)} async-done(((bf16[4,48,1536]{2,1,0:T(8,128)(2,1)}), bf16[4,48,1536]{2,1,0:T(8,128)(2,1)S(1)}, u32[]{:S(2)}, u32[]{:S(2)}) %all-to-all-start.2) | async-done | bytes 589856 | tf_op jit(solution)/shard_map/all_to_all | solution.py:146
  (160 shorter events, 58.9 us)
Async XLA Ops:
  7.2 78.5 %all-gather.2.cloned.1.call-start = ((), (), s32[]{:S(2)}) async-start(), calls=%async_computation.6 | async-start | bytes 1769472 | tf_op jit(solution)/shard_map/all_gather | solution.py:72
  14.7 26.1 %all-to-all-start = ((bf16[8,80,128]{2,1,0:T(8,128)(2,1)}), bf16[8,80,128]{2,1,0:T(8,128)(2,1)S(1)}, u32[]{:S(2)}, u32[]{:S(2)}) async-start(bf16[8,80,128]{2,1,0:T(8,128)(2,1)} %pad_maximum_fusion.5), calls=%async_computation | async-start | bytes 327680 | tf_op jit(solution)/shard_map/all_to_all | solution.py:28
  24.4 6.9 %collective-permute-start.1 = (bf16[32,1536]{1,0:T(8,128)(2,1)S(1)}, bf16[32,1536]{1,0:T(8,128)(2,1)S(1)}, u32[]{:S(2)}, u32[]{:S(2)}) collective-permute-start(bf16[32,1536]{1,0:T(8,128)(2,1)S(1)} %bitcast.208), channel_id=1, source_target_pairs={{0,192},{64,0},{128,64},{192,128},{1,193},{65,1},{129,65},{193,129... | collective-permute-start | bytes 294920 | tf_op jit(solution)/shard_map/ppermute | solution.py:17
  28.3 6.7 %collective-permute-start.3 = (bf16[32,1536]{1,0:T(8,128)(2,1)S(1)}, bf16[32,1536]{1,0:T(8,128)(2,1)S(1)}, u32[]{:S(2)}, u32[]{:S(2)}) collective-permute-start(bf16[32,1536]{1,0:T(8,128)(2,1)S(1)} %bitcast.210), channel_id=1, source_target_pairs={{0,64},{64,128},{128,192},{192,0},{1,65},{65,129},{129,193},{193,1... | collective-permute-start | bytes 294920 | tf_op jit(solution)/shard_map/ppermute | solution.py:17
  35.0 14.0 %collective-permute-start.6 = (bf16[4,32,1536]{2,1,0:T(8,128)(2,1)S(1)}, bf16[4,32,1536]{2,1,0:T(8,128)(2,1)}, u32[]{:S(2)}, u32[]{:S(2)}) collective-permute-start(bf16[4,32,1536]{2,1,0:T(8,128)(2,1)S(1)} %pad_maximum_fusion.4), channel_id=1, source_target_pairs={{0,2},{2,4},{4,6},{6,0},{1,3},{3,5},{5,7},{7,1},{8,10},{10,12},{12... | collective-permute-start | bytes 1179656 | tf_op jit(solution)/shard_map/ppermute | solution.py:17
  36.5 18.3 %collective-permute-start.5 = (bf16[4,32,1536]{2,1,0:T(8,128)(2,1)S(1)}, bf16[4,32,1536]{2,1,0:T(8,128)(2,1)}, u32[]{:S(2)}, u32[]{:S(2)}) collective-permute-start(bf16[4,32,1536]{2,1,0:T(8,128)(2,1)S(1)} %pad_maximum_fusion.4), channel_id=1, source_target_pairs={{0,4},{2,6},{4,0},{6,2},{1,5},{3,7},{5,1},{7,3},{8,12},{10,14},{12... | collective-permute-start | bytes 1179656 | tf_op jit(solution)/shard_map/ppermute | solution.py:17
  39.3 15.6 %collective-permute-start.4 = (bf16[4,32,1536]{2,1,0:T(8,128)(2,1)S(1)}, bf16[4,32,1536]{2,1,0:T(8,128)(2,1)}, u32[]{:S(2)}, u32[]{:S(2)}) collective-permute-start(bf16[4,32,1536]{2,1,0:T(8,128)(2,1)S(1)} %pad_maximum_fusion.4), channel_id=1, source_target_pairs={{0,6},{2,0},{4,2},{6,4},{1,7},{3,1},{5,3},{7,5},{8,14},{10,8},{12,... | collective-permute-start | bytes 1179656 | tf_op jit(solution)/shard_map/ppermute | solution.py:17
  54.9 14.8 %all-to-all-start.1 = ((bf16[8,64,128]{2,1,0:T(8,128)(2,1)}), bf16[8,64,128]{2,1,0:T(8,128)(2,1)S(1)}, u32[]{:S(2)}, u32[]{:S(2)}) async-start(bf16[8,64,128]{2,1,0:T(8,128)(2,1)} %add_convert_fusion.3), calls=%async_computation.1 | async-start | bytes 262144 | tf_op jit(solution)/shard_map/all_to_all | solution.py:49
  62.1 90.1 %reduce-scatter.2.cloned.1.call-start = ((), (), s32[]{:S(2)}) async-start(), calls=%async_computation.7 | async-start | bytes 1769472 | tf_op jit(solution)/shard_map/reduce_scatter | solution.py:133
  63.5 24.7 %collective-permute-start.7 = (bf16[512,1536]{1,0:T(8,128)(2,1)S(1)}, bf16[512,1536]{1,0:T(8,128)(2,1)}, u32[]{:S(2)}, u32[]{:S(2)}) collective-permute-start(bf16[512,1536]{1,0:T(8,128)(2,1)S(1)} %bitcast.170), channel_id=1, source_target_pairs={{0,1},{1,0},{2,3},{3,2},{4,5},{5,4},{6,7},{7,6},{8,9},{9,8},{10,11... | collective-permute-start | bytes 4718600 | tf_op jit(solution)/shard_map/ppermute | solution.py:90
  70.5 8.2 %collective-permute-start.8 = (bf16[2,4,32,512]{3,2,0,1:T(8,128)(2,1)S(1)}, bf16[2,4,32,512]{3,2,0,1:T(8,128)(2,1)S(1)}, u32[]{:S(2)}, u32[]{:S(2)}) collective-permute-start(bf16[2,4,32,512]{3,2,0,1:T(8,128)(2,1)S(1)} %fusion.30), channel_id=1, source_target_pairs={{0,192},{64,0},{128,64},{192,128},{1,193},{65,1},{129,65},{193,129... | collective-permute-start | bytes 786440 | tf_op jit(solution)/shard_map/ppermute | solution.py:17
  71.3 9.6 %collective-permute-start.9 = (bf16[2,4,32,512]{3,2,0,1:T(8,128)(2,1)S(1)}, bf16[2,4,32,512]{3,2,0,1:T(8,128)(2,1)}, u32[]{:S(2)}, u32[]{:S(2)}) collective-permute-start(bf16[2,4,32,512]{3,2,0,1:T(8,128)(2,1)S(1)} %fusion.30), channel_id=1, source_target_pairs={{0,128},{64,192},{128,0},{192,64},{1,129},{65,193},{129,1},{193,65... | collective-permute-start | bytes 786440 | tf_op jit(solution)/shard_map/ppermute | solution.py:17
  72.6 10.9 %collective-permute-start.10 = (bf16[2,4,32,512]{3,2,0,1:T(8,128)(2,1)S(1)}, bf16[2,4,32,512]{3,2,0,1:T(8,128)(2,1)}, u32[]{:S(2)}, u32[]{:S(2)}) collective-permute-start(bf16[2,4,32,512]{3,2,0,1:T(8,128)(2,1)S(1)} %fusion.30), channel_id=1, source_target_pairs={{0,64},{64,128},{128,192},{192,0},{1,65},{65,129},{129,193},{193,1... | collective-permute-start | bytes 786440 | tf_op jit(solution)/shard_map/ppermute | solution.py:17
  91.6 13.5 %collective-permute-start.15 = (bf16[2,4,32,512]{3,2,0,1:T(8,128)(2,1)}, bf16[2,4,32,512]{3,2,0,1:T(8,128)(2,1)}, u32[]{:S(2)}, u32[]{:S(2)}) collective-permute-start(bf16[2,4,32,512]{3,2,0,1:T(8,128)(2,1)} %get-tuple-element.46), channel_id=1, source_target_pairs={{0,64},{64,128},{128,192},{192,0},{1,65},{65,129},{129,193},{193,1... | collective-permute-start | bytes 786440 | tf_op jit(solution)/shard_map/ppermute | solution.py:17
  91.8 13.3 %collective-permute-start.17 = (bf16[2,4,32,512]{3,2,0,1:T(8,128)(2,1)}, bf16[2,4,32,512]{3,2,0,1:T(8,128)(2,1)}, u32[]{:S(2)}, u32[]{:S(2)}) collective-permute-start(bf16[2,4,32,512]{3,2,0,1:T(8,128)(2,1)} %get-tuple-element.47), channel_id=1, source_target_pairs={{0,192},{64,0},{128,64},{192,128},{1,193},{65,1},{129,65},{193,129... | collective-permute-start | bytes 786440 | tf_op jit(solution)/shard_map/ppermute | solution.py:17
  94.9 10.3 %collective-permute-start.16 = (bf16[2,4,32,512]{3,2,0,1:T(8,128)(2,1)}, bf16[2,4,32,512]{3,2,0,1:T(8,128)(2,1)}, u32[]{:S(2)}, u32[]{:S(2)}) collective-permute-start(bf16[2,4,32,512]{3,2,0,1:T(8,128)(2,1)} %get-tuple-element.48), channel_id=1, source_target_pairs={{0,128},{64,192},{128,0},{192,64},{1,129},{65,193},{129,1},{193,65... | collective-permute-start | bytes 786440 | tf_op jit(solution)/shard_map/ppermute | solution.py:17
  104.8 21.6 %collective-permute-start.11 = (bf16[512,1536]{1,0:T(8,128)(2,1)}, bf16[512,1536]{1,0:T(8,128)(2,1)}, u32[]{:S(2)}, u32[]{:S(2)}) collective-permute-start(bf16[512,1536]{1,0:T(8,128)(2,1)} %convolution_convert_fusion), channel_id=1, source_target_pairs={{0,1},{1,0},{2,3},{3,2},{4,5},{5,4},{6,7},{7,6},{8,9},{9,8},{10,11... | collective-permute-start | bytes 4718600 | tf_op jit(solution)/shard_map/ppermute | solution.py:134
  108.6 15.4 %all-to-all-start.3 = ((bf16[8,64,128]{2,1,0:T(8,128)(2,1)}), bf16[8,64,128]{2,1,0:T(8,128)(2,1)S(1)}, u32[]{:S(2)}, u32[]{:S(2)}) async-start(bf16[8,64,128]{2,1,0:T(8,128)(2,1)} %bitcast.43), calls=%async_computation.4 | async-start | bytes 262144 | tf_op jit(solution)/shard_map/all_to_all | solution.py:28
  124.1 11.3 %collective-permute-start.18 = (bf16[80,128]{1,0:T(8,128)(2,1)S(1)}, bf16[80,128]{1,0:T(8,128)(2,1)S(1)}, u32[]{:S(2)}, u32[]{:S(2)}) collective-permute-start(bf16[80,128]{1,0:T(8,128)(2,1)S(1)} %concatenate.32), channel_id=1, source_target_pairs={{64,0},{128,64},{192,128},{65,1},{129,65},{193,129},{66,2},{130,66... | collective-permute-start | bytes 61448 | tf_op jit(solution)/shard_map/ppermute | solution.py:44
  130.2 13.2 %collective-permute-start.12 = (bf16[128,1536]{1,0:T(8,128)(2,1)}, bf16[128,1536]{1,0:T(8,128)(2,1)}, u32[]{:S(2)}, u32[]{:S(2)}) collective-permute-start(bf16[128,1536]{1,0:T(8,128)(2,1)} %get-tuple-element.43), channel_id=1, source_target_pairs={{0,2},{2,4},{4,6},{6,0},{1,3},{3,5},{5,7},{7,1},{8,10},{10,12},{12... | collective-permute-start | bytes 1179656 | tf_op jit(solution)/shard_map/ppermute | solution.py:17
  132.3 16.1 %collective-permute-start.14 = (bf16[128,1536]{1,0:T(8,128)(2,1)S(1)}, bf16[128,1536]{1,0:T(8,128)(2,1)}, u32[]{:S(2)}, u32[]{:S(2)}) collective-permute-start(bf16[128,1536]{1,0:T(8,128)(2,1)S(1)} %get-tuple-element.44), channel_id=1, source_target_pairs={{0,6},{2,0},{4,2},{6,4},{1,7},{3,1},{5,3},{7,5},{8,14},{10,8},{12,... | collective-permute-start | bytes 1179656 | tf_op jit(solution)/shard_map/ppermute | solution.py:17
  134.0 16.6 %collective-permute-start.13 = (bf16[128,1536]{1,0:T(8,128)(2,1)S(1)}, bf16[128,1536]{1,0:T(8,128)(2,1)}, u32[]{:S(2)}, u32[]{:S(2)}) collective-permute-start(bf16[128,1536]{1,0:T(8,128)(2,1)S(1)} %get-tuple-element.45), channel_id=1, source_target_pairs={{0,4},{2,6},{4,0},{6,2},{1,5},{3,7},{5,1},{7,3},{8,12},{10,14},{12... | collective-permute-start | bytes 1179656 | tf_op jit(solution)/shard_map/ppermute | solution.py:17
  138.3 15.7 %all-to-all-start.4 = ((bf16[8,64,128]{2,1,0:T(8,128)(2,1)}), bf16[8,64,128]{2,1,0:T(8,128)(2,1)S(1)}, u32[]{:S(2)}, u32[]{:S(2)}) async-start(bf16[8,64,128]{2,1,0:T(8,128)(2,1)} %add_convert_fusion.2), calls=%async_computation.5 | async-start | bytes 262144 | tf_op jit(solution)/shard_map/all_to_all | solution.py:49
  154.1 15.7 %all-to-all-start.2 = ((bf16[4,48,1536]{2,1,0:T(8,128)(2,1)}), bf16[4,48,1536]{2,1,0:T(8,128)(2,1)S(1)}, u32[]{:S(2)}, u32[]{:S(2)}) async-start(bf16[4,48,1536]{2,1,0:T(8,128)(2,1)} %pad_maximum_fusion.3), calls=%async_computation.3 | async-start | bytes 1179648 | tf_op jit(solution)/shard_map/all_to_all | solution.py:146
  (23 other events, 197.2 us)
Sparse Core Ops, SparseCore 0:
  9.8 44.3 all-gather.1
  100.1 40.5 reduce-scatter.1

commit v3 on v2

--- a/solution.py
+++ b/solution.py
@@ -59,6 +59,8 @@
     half = nx * ny * sub
     core = lax.axis_index("c")
 
+    weight_here, key_rows = lax.optimization_barrier((out_weight.T, key_rows))
+    weight_t = lax.all_gather(weight_here, "z", axis=0, tiled=True)
     query_heads = queries.reshape(tok, heads, HD)
     key_heads = key_rows.reshape(tok, heads, HD)
     value_heads = value_rows.reshape(tok, heads, HD)
@@ -69,25 +71,29 @@
     in_first = (docs == first_doc)[:, None, None]
     in_last = (docs == last_doc)[:, None, None]
 
-    weight_t = lax.all_gather(out_weight.T, "z", axis=0, tiled=True)
     pieces = out_grad.reshape(sub, ny, cols).transpose(1, 0, 2)
+    key_last = jnp.where(in_last, key_heads, jnp.zeros_like(key_heads))
+    local_state = jnp.einsum("thd,the->hde", key_last, value_heads, preferred_element_type=F32)
+    pieces, local_state = lax.optimization_barrier((pieces, local_state.astype(BF)))
     row, place = lax.axis_index("y"), lax.axis_index("x")
     piece = [lax.dynamic_index_in_dim(pieces, row, 0, False)]
     for step in range(1, ny):
         sent = lax.dynamic_index_in_dim(pieces, (row - step) % ny, 0, False)
         piece.append(turn(sent, "y", -step))
-    piece = jnp.stack(piece)
-
-    key_last = jnp.where(in_last, key_heads, jnp.zeros_like(key_heads))
-    local_state = jnp.einsum("thd,the->hde", key_last, value_heads, preferred_element_type=F32)
+    piece = jnp.stack(piece + piece)
+    piece = lax.dynamic_slice_in_dim(piece, (ny - row) % ny, ny, 0)
     ones = jnp.ones((8, HD), F32)
     marks = jnp.concatenate([ones * (first_doc + 1.0), ones * (last_doc + 1.0)]).astype(BF)
     og_own = [piece] + [turn(piece, "x", -step) for step in range(1, nx)]
-    prior, first_marks, last_marks, og_own = row_state(
-        local_state.reshape(heads * HD, HD), None, None, marks, False, og_own
+    prior, first_marks, last_marks, (og_own, weight_t) = row_state(
+        local_state.reshape(heads * HD, HD), None, None, marks, False, (og_own, weight_t)
     )
     og_own = jnp.stack(og_own).reshape(half, cols)
     og_other = lax.ppermute(og_own, "c", SWAP)
+    gn_part = jnp.stack(
+        [jnp.dot(g, weight_t, preferred_element_type=F32).astype(BF) for g in (og_own, og_other)]
+    )
+    gn_part = gn_part.reshape(2, nx, ny, sub, width).transpose(2, 0, 1, 3, 4)
     prior = prior.reshape(heads, HD, HD)
 
     scores = jnp.einsum("thd,shd->hts", query_heads, key_heads, preferred_element_type=F32)
@@ -103,20 +109,13 @@
     by_core = jnp.where(core == 0, by_core, by_core[::-1])
     by_core = jnp.concatenate([by_core, by_core], axis=1)
     by_core = lax.dynamic_slice_in_dim(by_core, place, nx, 1)
-    gn_part = jnp.stack(
-        [jnp.dot(g, weight_t, preferred_element_type=F32).astype(BF) for g in (og_own, og_other)]
-    )
-    gn_part = gn_part.reshape(2, nx, ny, sub, width).transpose(2, 0, 1, 3, 4)
-    normed_all = [by_core] + [turn(by_core, "y", -step) for step in range(1, ny)]
-    normed_all = jnp.stack(normed_all, axis=2).reshape(2, half, width)
-    gn_part, normed_all = lax.optimization_barrier((gn_part, normed_all))
-
-    gn = gn_part[0].astype(F32)
-    for step in range(1, ny):
-        gn = gn + turn(gn_part[step], "y", step).astype(F32)
-    gn = lax.dynamic_slice_in_dim(jnp.concatenate([gn, gn], axis=1), (nx - place) % nx, nx, 1)
-    gn = jnp.where(core == 0, gn, gn[::-1])
-    grad_normed = gn.transpose(1, 0, 2, 3).reshape(tok, heads, HD)
+    by_core = jnp.broadcast_to(by_core[None], (ny,) + by_core.shape)
+    normed_all = lax.all_to_all(by_core, "y", 0, 0).transpose(1, 2, 0, 3, 4)
+    normed_all = normed_all.reshape(2, half, width)
+    gn = lax.psum_scatter(
+        gn_part.reshape(ny * tok, width), "y", scatter_dimension=0, tiled=True
+    )
+    gn, normed_all = lax.optimization_barrier((gn, normed_all))
 
     def project(rows):
         return lax.dot_general(
@@ -130,30 +129,42 @@
     )
     rows = width // (ny * nz)
     wg_part = wg_part.astype(BF).reshape(ny, nz, rows, cols).transpose(1, 0, 2, 3)
-    wg_sum = lax.psum_scatter(wg_part.reshape(width, cols), "z", scatter_dimension=0, tiled=True)
+    gn, normed_all, wg_part = lax.optimization_barrier(
+        (gn, normed_all, wg_part.reshape(width, cols))
+    )
+    gn = gn.astype(F32).reshape(2, nx, sub, width)
+    gn = lax.dynamic_slice_in_dim(jnp.concatenate([gn, gn], axis=1), (nx - place) % nx, nx, 1)
+    gn = jnp.where(core == 0, gn, gn[::-1])
+    grad_normed = gn.transpose(1, 0, 2, 3).reshape(tok, heads, HD)
+
+    mixed_grad = (
+        inv_norm * (grad_normed - normed * jnp.mean(grad_normed * normed, axis=-1, keepdims=True))
+    ).astype(BF)
+    query_first = jnp.where(in_first, query_heads, jnp.zeros_like(query_heads))
+    local_future = jnp.einsum("thd,the->hde", query_first, mixed_grad, preferred_element_type=F32)
+    wg_sum = lax.psum_scatter(wg_part, "z", scatter_dimension=0, tiled=True)
     out_sent = lax.ppermute(project(normed_all[1]).astype(BF), "c", SWAP)
+    out_sent, local_future = lax.optimization_barrier((out_sent, local_future.astype(BF)))
     out_own = (project(normed_all[0]) + out_sent.astype(F32)).astype(BF)
     out_own = out_own.reshape(nx, ny * sub, cols)
     out_sum = out_own[0].astype(F32)
     for step in range(1, nx):
         out_sum = out_sum + turn(out_own[step], "x", step).astype(F32)
     out_sum = out_sum.astype(BF).reshape(ny, sub, cols)
-    out_sum = jnp.concatenate([out_sum, out_sum])
-    out_sum = lax.dynamic_slice_in_dim(out_sum, (ny - row) % ny, ny, 0)
+    future, unused, unused, unused = row_state(
+        local_future.reshape(heads * HD, HD), first_marks, last_marks, None, True
+    )
     last = jnp.concatenate(
         [out_sum, wg_sum.reshape(ny, rows, cols)], axis=1
     )
-    last = lax.all_to_all(last, "y", 0, 0).transpose(1, 0, 2).reshape(sub + rows, ny * cols)
+    blocks = [None] * ny
+    for step in range(ny):
+        block = lax.dynamic_index_in_dim(last, (row + step) % ny, 0, False)
+        blocks[-step] = turn(block, "y", step) if step else block
+    last = lax.dynamic_slice_in_dim(jnp.stack(blocks + blocks), (ny - row) % ny, ny, 0)
+    last = last.transpose(1, 0, 2).reshape(sub + rows, ny * cols)
     layer_out, weight_grad = last[:sub], last[sub:]
 
-    mixed_grad = (
-        inv_norm * (grad_normed - normed * jnp.mean(grad_normed * normed, axis=-1, keepdims=True))
-    ).astype(BF)
-    query_first = jnp.where(in_first, query_heads, jnp.zeros_like(query_heads))
-    local_future = jnp.einsum("thd,the->hde", query_first, mixed_grad, preferred_element_type=F32)
-    future, unused, unused, unused = row_state(
-        local_future.reshape(heads * HD, HD), first_marks, last_marks, None, True
-    )
     future = future.reshape(heads, HD, HD)
 
     grad_raw = jnp.einsum("the,she->hts", mixed_grad, value_heads, preferred_element_type=F32)

time: 179 us -> 178 us (level)
  starting transfers between devices: 57.4 us -> 51.1 us
  local copies, waits for them, and re-layouts: 15.6 us -> 21.5 us
  other arithmetic: 18.1 us -> 14.6 us
  waiting for transfers between devices: 48.8 us -> 51.3 us
    ppermute x15 -> x12, waiting for transfers between devices: 28.3 us -> 13.4 us  [turn(): return lax.ppermute(x, axis, [(i, (i + by) % count) for i in range(count)])]
    all_to_all x1, waiting for transfers between devices: 6.74 us -> 21.6 us  [shards(): normed_all = lax.all_to_all(by_core, 'y', 0, 0).transpose(1, 2, 0, 3, 4)]
    ppermute x15 -> x12, starting transfers between devices: 22.8 us -> 15.1 us  [turn(): return lax.ppermute(x, axis, [(i, (i + by) % count) for i in range(count)])]
    ppermute x2, waiting for transfers between devices: 0.44 us -> 4.52 us  [row_state(): message = lax.ppermute(message, 'y', pairs)]
    all_to_all x1, starting transfers between devices: 6.73 us -> 3.54 us  [shards(): normed_all = lax.all_to_all(by_core, 'y', 0, 0).transpose(1, 2, 0, 3, 4)]
    ppermute x2, starting transfers between devices: 2.58 us -> 5.18 us  [row_state(): message = lax.ppermute(message, 'y', pairs)]
    another operation x2 -> x7, local copies, waits for them, and re-layouts: 1.85 us -> 4.37 us  [the longest x4 3.02 us: shards(): piece = jnp.stack(piece + piece)]
    concatenate x2 -> x0, other arithmetic: 2.01 us -> none  [the longest x1 1.85 us: shards(): last = jnp.concatenate([out_sum, wg_sum.reshape(ny, rows, cols)], axis=1)]
  transfers between devices with their start and end apart: 26 -> 24, of which waited for: 15 -> 13; matrix products, arithmetic and copies ran while one was open for 26% -> 21% of each run, Pallas kernels for 0% -> 0%
where the time goes in v3:
time: 178 us; the launch traced here: 177 us
  waiting for transfers between devices  51.3 us (29%)
  starting transfers between devices  51.1 us (29%)
  local copies, waits for them, and re-layouts  21.5 us (12%)
  matrix products  19.8 us (11%)
  between operations  18.5 us (10%)
  other arithmetic  14.6 us (8%)
    all_to_all x1, waiting for transfers between devices, shards(): normed_all = lax.all_to_all(by_core, 'y', 0, 0).transpose(1, 2, 0, 3, 4)  21.6 us
    all_to_all x2, starting transfers between devices, row_state(): got = lax.all_to_all(slices, 'z', 0, 0)  15.4 us
    ppermute x12, starting transfers between devices, turn(): return lax.ppermute(x, axis, [(i, (i + by) % count) for i in range(count)])  15.1 us
    ppermute x12, waiting for transfers between devices, turn(): return lax.ppermute(x, axis, [(i, (i + by) % count) for i in range(count)])  13.4 us
    all_to_all x2, starting transfers between devices, row_state(): out = lax.all_to_all(total, 'z', 0, 0)  11.7 us
    dot_general x2, matrix products, project(): lax.dot_general(rows, weight_t, (((1,), (1,)), ((), ())), preferred_eleme...  6.56 us
    unnamed x59, local copies, waits for them, and re-layouts  6.19 us
    all_to_all x2, waiting for transfers between devices, row_state(): out = lax.all_to_all(total, 'z', 0, 0)  5.77 us
  transfers between devices with their start and end apart: 24, of which 13 were waited for; matrix products, arithmetic and copies ran while one was open for 21% of the time, Pallas kernels for 0%

profile of v3, /device:TPU:32, one launch (start us, length us, event | category | flops | bytes accessed | tf_op | source)
XLA Modules:
  0.0 176.9 jit_solution(4524155605053680868)
XLA Ops:
  13.7 3.1 %collective-permute-start.1 = (bf16[32,1536]{1,0:T(8,128)(2,1)S(1)}, bf16[32,1536]{1,0:T(8,128)(2,1)S(1)}, u32[]{:S(2)}, u32[]{:S(2)}) collective-permute-start(bf16[32,1536]{1,0:T(8,128)(2,1)S(1)} %bitcast.213), channel_id=1, source_target_pairs={{0,192},{64,0},{128,64},{192,128},{1,193},{65,1},{129,65},{193,129... | collective-permute-start | bytes 294920 | tf_op jit(solution)/shard_map/ppermute | solution.py:17
  20.8 8.6 %all-to-all-start = ((bf16[8,80,128]{2,1,0:T(8,128)(2,1)}), bf16[8,80,128]{2,1,0:T(8,128)(2,1)S(1)}, u32[]{:S(2)}, u32[]{:S(2)}) async-start(bf16[8,80,128]{2,1,0:T(8,128)(2,1)} %pad_maximum_fusion.3), calls=%async_computation | async-start | bytes 327680 | tf_op jit(solution)/shard_map/all_to_all | solution.py:28
  29.9 2.6 %stack.61 = bf16[8,32,1536]{2,0,1:T(8,128)(2,1)S(1)} concatenate(bf16[1,32,1536]{2,0,1:T(2,128)(2,1)S(1)} %get-tuple-element.78, bf16[1,32,1536]{2,0,1:T(2,128)(2,1)S(1)} %copy.169, bf16[1,32,1536]{2,0,1:T(2,128)(2,1)S(1)} %copy.170, bf16[1,32,1536]{2,0,1:T(2,128)(2,1)S(1)} %copy.171, bf16[1,32,1536]{2,0,1:T(2,128)(2,1)S(1)} %get-tuple-element.78, ...), dimensions={0} | concatenate | bytes 1572864 | tf_op jit(solution)/shard_map/stack | solution.py:83
  32.7 2.8 %collective-permute-start.4 = (bf16[4,32,1536]{2,0,1:T(4,128)(2,1)S(1)}, bf16[4,32,1536]{2,0,1:T(4,128)(2,1)S(1)}, u32[]{:S(2)}, u32[]{:S(2)}) collective-permute-start(bf16[4,32,1536]{2,0,1:T(4,128)(2,1)S(1)} %constant_dynamic-slice_fusion.1), channel_id=1, source_target_pairs={{0,6},{2,0},{4,2},{6,4},{1,7},{3,1},{5,3},{7,5},{8,14},{10,8},{12,... | collective-permute-start | bytes 1179656 | tf_op jit(solution)/shard_map/ppermute | solution.py:17
  37.2 2.3 %all-to-all-done = bf16[8,80,128]{2,1,0:T(8,128)(2,1)S(1)} async-done(((bf16[8,80,128]{2,1,0:T(8,128)(2,1)}), bf16[8,80,128]{2,1,0:T(8,128)(2,1)S(1)}, u32[]{:S(2)}, u32[]{:S(2)}) %all-to-all-start) | async-done | bytes 163872 | tf_op jit(solution)/shard_map/all_to_all | solution.py:28
  41.7 3.9 %collective-permute-start = (bf16[80,128]{1,0:T(8,128)(2,1)S(1)}, bf16[80,128]{1,0:T(8,128)(2,1)S(1)}, u32[]{:S(2)}, u32[]{:S(2)}) collective-permute-start(bf16[80,128]{1,0:T(8,128)(2,1)S(1)} %concatenate.27), channel_id=1, source_target_pairs={{0,64},{64,128},{128,192},{1,65},{65,129},{129,193},{2,66},{66,130... | collective-permute-start | bytes 61448 | tf_op jit(solution)/shard_map/ppermute | solution.py:44
  50.9 3.7 %collective-permute-done.6 = bf16[4,32,1536]{2,0,1:T(4,128)(2,1)S(1)} collective-permute-done((bf16[4,32,1536]{2,0,1:T(4,128)(2,1)S(1)}, bf16[4,32,1536]{2,0,1:T(4,128)(2,1)S(1)}, u32[]{:S(2)}, u32[]{:S(2)}) %collective-permute-start.6) | collective-permute-done | bytes 393248 | tf_op jit(solution)/shard_map/ppermute | solution.py:17
  58.2 7.2 %all-to-all-start.1 = ((bf16[8,64,128]{2,1,0:T(8,128)(2,1)}), bf16[8,64,128]{2,1,0:T(8,128)(2,1)S(1)}, u32[]{:S(2)}, u32[]{:S(2)}) async-start(bf16[8,64,128]{2,1,0:T(8,128)(2,1)} %add_convert_fusion.2), calls=%async_computation.2 | async-start | bytes 262144 | tf_op jit(solution)/shard_map/all_to_all | solution.py:49
  65.5 2.5 %convolution_convert_fusion.2 = bf16[512,512]{1,0:T(8,128)(2,1)S(1)} fusion(bf16[512,1536]{1,0:T(8,128)(2,1)S(1)} %bitcast.175, bf16[1536,512]{1,0:T(8,128)(2,1)} %all-gather.2.cloned.1.call-done), kind=kOutput, calls=%fused_computation.12 | convolution fusion | flops 805568512 | bytes 3670016 | tf_op jit(solution)/shard_map/dot_general | solution.py:94
  68.0 2.4 %convolution_convert_fusion.1 = bf16[512,512]{1,0:T(8,128)(2,1)S(1)} fusion(bf16[512,1536]{1,0:T(8,128)(2,1)} %collective-permute-done.7, bf16[1536,512]{1,0:T(8,128)(2,1)S(1)} %copy-done.22), kind=kOutput, calls=%fused_computation.11 | convolution fusion | flops 805568512 | bytes 3670016 | tf_op jit(solution)/shard_map/dot_general | solution.py:94
  75.3 3.5 %all-to-all-start.2 = ((bf16[4,2,4,32,512]{4,3,2,1,0:T(8,128)(2,1)}), bf16[4,2,4,32,512]{4,3,2,1,0:T(8,128)(2,1)S(1)}, u32[]{:S(2)}, u32[]{:S(2)}) async-start(bf16[4,2,4,32,512]{4,3,2,1,0:T(8,128)(2,1)} %broadcast_in_dim.196), calls=%async_computation.3 | async-start | bytes 2097152 | tf_op jit(solution)/shard_map/all_to_all | solution.py:113
  79.5 21.6 %all-to-all-done.2 = bf16[4,2,4,32,512]{4,3,2,1,0:T(8,128)(2,1)S(1)} async-done(((bf16[4,2,4,32,512]{4,3,2,1,0:T(8,128)(2,1)}), bf16[4,2,4,32,512]{4,3,2,1,0:T(8,128)(2,1)S(1)}, u32[]{:S(2)}, u32[]{:S(2)}) %all-to-all-start.2) | async-done | bytes 1048608 | tf_op jit(solution)/shard_map/all_to_all | solution.py:113
  102.2 2.1 %fusion.18 = f32[512,1536]{1,0:T(8,128)S(1)} fusion(bf16[512,1536]{1,0:T(8,128)(2,1)S(1)} %bitcast.176, bf16[2,512,512]{2,1,0:T(8,128)(2,1)} %bitcast.179), kind=kOutput, calls=%fused_computation.51 | convolution fusion | flops 805306368 | bytes 5242880 | tf_op jit(solution)/shard_map/dot_general | solution.py:125
  104.4 2.4 %fusion = bf16[512,1536]{1,0:T(8,128)(2,1)S(1)} fusion(f32[512,1536]{1,0:T(8,128)S(1)} %fusion.18, bf16[512,1536]{1,0:T(8,128)(2,1)} %collective-permute-done.7, bf16[2,512,512]{2,1,0:T(8,128)(2,1)S(1)} %bitcast.180), kind=kOutput, calls=%fused_computation.3 | convolution fusion | flops 806879232 | bytes 6815744 | tf_op jit(solution)/shard_map/dot_general | solution.py:127
  108.8 3.7 %convolution_convert_fusion = bf16[512,1536]{1,0:T(8,128)(2,1)} fusion(bf16[1536,512]{1,0:T(8,128)(2,1)} %all-gather.2.cloned.1.call-done, bf16[2,512,512]{2,1,0:T(8,128)(2,1)S(1)} %bitcast.181), kind=kOutput, calls=%fused_computation.2 | convolution fusion | flops 806092800 | bytes 3670016 | tf_op jit(solution)/shard_map/dot_general | solution.py:121
  116.8 6.8 %all-to-all-start.3 = ((bf16[8,64,128]{2,1,0:T(8,128)(2,1)}), bf16[8,64,128]{2,1,0:T(8,128)(2,1)S(1)}, u32[]{:S(2)}, u32[]{:S(2)}) async-start(bf16[8,64,128]{2,1,0:T(8,128)(2,1)} %bitcast.47), calls=%async_computation.5 | async-start | bytes 262144 | tf_op jit(solution)/shard_map/all_to_all | solution.py:28
  123.7 2.9 %fusion.1 = bf16[512,1536]{1,0:T(8,128)(2,1)S(1)} fusion(bf16[512,1536]{1,0:T(8,128)(2,1)} %collective-permute-done.8, bf16[1536,512]{1,0:T(8,128)(2,1)} %all-gather.2.cloned.1.call-done, bf16[2,512,512]{2,1,0:T(8,128)(2,1)S(1)} %bitcast.182), kind=kOutput, calls=%fused_computation.4 | convolution fusion | flops 807665664 | bytes 5242880 | tf_op jit(solution)/shard_map/dot_general | solution.py:121
  130.3 3.0 %all-to-all-done.3 = bf16[8,64,128]{2,1,0:T(8,128)(2,1)S(1)} async-done(((bf16[8,64,128]{2,1,0:T(8,128)(2,1)}), bf16[8,64,128]{2,1,0:T(8,128)(2,1)S(1)}, u32[]{:S(2)}, u32[]{:S(2)}) %all-to-all-start.3) | async-done | bytes 131104 | tf_op jit(solution)/shard_map/all_to_all | solution.py:28
  135.0 4.1 %collective-permute-done.15 = bf16[80,128]{1,0:T(8,128)(2,1)S(1)} collective-permute-done((bf16[80,128]{1,0:T(8,128)(2,1)S(1)}, bf16[80,128]{1,0:T(8,128)(2,1)S(1)}, u32[]{:S(2)}, u32[]{:S(2)}) %collective-permute-start.15) | collective-permute-done | bytes 20512 | tf_op jit(solution)/shard_map/ppermute | solution.py:44
  142.0 4.5 %all-to-all-start.4 = ((bf16[8,64,128]{2,1,0:T(8,128)(2,1)}), bf16[8,64,128]{2,1,0:T(8,128)(2,1)S(1)}, u32[]{:S(2)}, u32[]{:S(2)}) async-start(bf16[8,64,128]{2,1,0:T(8,128)(2,1)} %add_convert_fusion.1), calls=%async_computation.6 | async-start | bytes 262144 | tf_op jit(solution)/shard_map/all_to_all | solution.py:49
  150.0 4.3 %all-to-all-done.4 = bf16[8,64,128]{2,1,0:T(8,128)(2,1)S(1)} async-done(((bf16[8,64,128]{2,1,0:T(8,128)(2,1)}), bf16[8,64,128]{2,1,0:T(8,128)(2,1)S(1)}, u32[]{:S(2)}, u32[]{:S(2)}) %all-to-all-start.4) | async-done | bytes 131104 | tf_op jit(solution)/shard_map/all_to_all | solution.py:49
  157.1 2.3 %collective-permute-start.12 = (bf16[48,1536]{1,0:T(8,128)(2,1)}, bf16[48,1536]{1,0:T(8,128)(2,1)S(1)}, u32[]{:S(2)}, u32[]{:S(2)}) collective-permute-start(bf16[48,1536]{1,0:T(8,128)(2,1)} %get-tuple-element.73), channel_id=1, source_target_pairs={{0,192},{64,0},{128,64},{192,128},{1,193},{65,1},{129,65},{193,129... | collective-permute-start | bytes 442376 | tf_op jit(solution)/shard_map/ppermute | solution.py:17
  161.4 2.6 %collective-permute-done.12 = bf16[48,1536]{1,0:T(8,128)(2,1)S(1)} collective-permute-done((bf16[48,1536]{1,0:T(8,128)(2,1)}, bf16[48,1536]{1,0:T(8,128)(2,1)S(1)}, u32[]{:S(2)}, u32[]{:S(2)}) %collective-permute-start.12) | collective-permute-done | bytes 147488 | tf_op jit(solution)/shard_map/ppermute | solution.py:17
  164.0 3.2 %collective-permute-done.13 = bf16[48,1536]{1,0:T(8,128)(2,1)S(1)} collective-permute-done((bf16[48,1536]{1,0:T(8,128)(2,1)S(1)}, bf16[48,1536]{1,0:T(8,128)(2,1)S(1)}, u32[]{:S(2)}, u32[]{:S(2)}) %collective-permute-start.13) | collective-permute-done | bytes 147488 | tf_op jit(solution)/shard_map/ppermute | solution.py:17
  (172 shorter events, 52.1 us)
Async XLA Ops:
  7.2 47.4 %all-gather.2.cloned.1.call-start = ((), (), s32[]{:S(2)}) async-start(), calls=%async_computation.7 | async-start | bytes 1769472 | tf_op jit(solution)/shard_map/all_gather | solution.py:63
  13.7 15.6 %collective-permute-start.1 = (bf16[32,1536]{1,0:T(8,128)(2,1)S(1)}, bf16[32,1536]{1,0:T(8,128)(2,1)S(1)}, u32[]{:S(2)}, u32[]{:S(2)}) collective-permute-start(bf16[32,1536]{1,0:T(8,128)(2,1)S(1)} %bitcast.213), channel_id=1, source_target_pairs={{0,192},{64,0},{128,64},{192,128},{1,193},{65,1},{129,65},{193,129... | collective-permute-start | bytes 294920 | tf_op jit(solution)/shard_map/ppermute | solution.py:17
  16.9 12.7 %collective-permute-start.2 = (bf16[32,1536]{1,0:T(8,128)(2,1)S(1)}, bf16[32,1536]{1,0:T(8,128)(2,1)S(1)}, u32[]{:S(2)}, u32[]{:S(2)}) collective-permute-start(bf16[32,1536]{1,0:T(8,128)(2,1)S(1)} %bitcast.215), channel_id=1, source_target_pairs={{0,128},{64,192},{128,0},{192,64},{1,129},{65,193},{129,1},{193,65... | collective-permute-start | bytes 294920 | tf_op jit(solution)/shard_map/ppermute | solution.py:17
  17.6 12.1 %collective-permute-start.3 = (bf16[32,1536]{1,0:T(8,128)(2,1)S(1)}, bf16[32,1536]{1,0:T(8,128)(2,1)S(1)}, u32[]{:S(2)}, u32[]{:S(2)}) collective-permute-start(bf16[32,1536]{1,0:T(8,128)(2,1)S(1)} %bitcast.217), channel_id=1, source_target_pairs={{0,64},{64,128},{128,192},{192,0},{1,65},{65,129},{129,193},{193,1... | collective-permute-start | bytes 294920 | tf_op jit(solution)/shard_map/ppermute | solution.py:17
  20.8 18.7 %all-to-all-start = ((bf16[8,80,128]{2,1,0:T(8,128)(2,1)}), bf16[8,80,128]{2,1,0:T(8,128)(2,1)S(1)}, u32[]{:S(2)}, u32[]{:S(2)}) async-start(bf16[8,80,128]{2,1,0:T(8,128)(2,1)} %pad_maximum_fusion.3), calls=%async_computation | async-start | bytes 327680 | tf_op jit(solution)/shard_map/all_to_all | solution.py:28
  32.7 18.3 %collective-permute-start.4 = (bf16[4,32,1536]{2,0,1:T(4,128)(2,1)S(1)}, bf16[4,32,1536]{2,0,1:T(4,128)(2,1)S(1)}, u32[]{:S(2)}, u32[]{:S(2)}) collective-permute-start(bf16[4,32,1536]{2,0,1:T(4,128)(2,1)S(1)} %constant_dynamic-slice_fusion.1), channel_id=1, source_target_pairs={{0,6},{2,0},{4,2},{6,4},{1,7},{3,1},{5,3},{7,5},{8,14},{10,8},{12,... | collective-permute-start | bytes 1179656 | tf_op jit(solution)/shard_map/ppermute | solution.py:17
  35.5 15.4 %collective-permute-start.5 = (bf16[4,32,1536]{2,0,1:T(4,128)(2,1)S(1)}, bf16[4,32,1536]{2,0,1:T(4,128)(2,1)S(1)}, u32[]{:S(2)}, u32[]{:S(2)}) collective-permute-start(bf16[4,32,1536]{2,0,1:T(4,128)(2,1)S(1)} %constant_dynamic-slice_fusion.1), channel_id=1, source_target_pairs={{0,4},{2,6},{4,0},{6,2},{1,5},{3,7},{5,1},{7,3},{8,12},{10,14},{12... | collective-permute-start | bytes 1179656 | tf_op jit(solution)/shard_map/ppermute | solution.py:17
  36.3 18.3 %collective-permute-start.6 = (bf16[4,32,1536]{2,0,1:T(4,128)(2,1)S(1)}, bf16[4,32,1536]{2,0,1:T(4,128)(2,1)S(1)}, u32[]{:S(2)}, u32[]{:S(2)}) collective-permute-start(bf16[4,32,1536]{2,0,1:T(4,128)(2,1)S(1)} %constant_dynamic-slice_fusion.1), channel_id=1, source_target_pairs={{0,2},{2,4},{4,6},{6,0},{1,3},{3,5},{5,7},{7,1},{8,10},{10,12},{12... | collective-permute-start | bytes 1179656 | tf_op jit(solution)/shard_map/ppermute | solution.py:17
  41.7 5.4 %collective-permute-start = (bf16[80,128]{1,0:T(8,128)(2,1)S(1)}, bf16[80,128]{1,0:T(8,128)(2,1)S(1)}, u32[]{:S(2)}, u32[]{:S(2)}) collective-permute-start(bf16[80,128]{1,0:T(8,128)(2,1)S(1)} %concatenate.27), channel_id=1, source_target_pairs={{0,64},{64,128},{128,192},{1,65},{65,129},{129,193},{2,66},{66,130... | collective-permute-start | bytes 61448 | tf_op jit(solution)/shard_map/ppermute | solution.py:44
  56.4 11.6 %collective-permute-start.7 = (bf16[512,1536]{1,0:T(8,128)(2,1)S(1)}, bf16[512,1536]{1,0:T(8,128)(2,1)}, u32[]{:S(2)}, u32[]{:S(2)}) collective-permute-start(bf16[512,1536]{1,0:T(8,128)(2,1)S(1)} %bitcast.174), channel_id=1, source_target_pairs={{0,1},{1,0},{2,3},{3,2},{4,5},{5,4},{6,7},{7,6},{8,9},{9,8},{10,11... | collective-permute-start | bytes 4718600 | tf_op jit(solution)/shard_map/ppermute | solution.py:92
  58.2 15.0 %all-to-all-start.1 = ((bf16[8,64,128]{2,1,0:T(8,128)(2,1)}), bf16[8,64,128]{2,1,0:T(8,128)(2,1)S(1)}, u32[]{:S(2)}, u32[]{:S(2)}) async-start(bf16[8,64,128]{2,1,0:T(8,128)(2,1)} %add_convert_fusion.2), calls=%async_computation.2 | async-start | bytes 262144 | tf_op jit(solution)/shard_map/all_to_all | solution.py:49
  65.5 36.7 %reduce-scatter.3.cloned.1.call-start = ((), (), s32[]{:S(2)}) async-start(), calls=%async_computation.8 | async-start | bytes 1310720 | tf_op jit(solution)/shard_map/reduce_scatter | solution.py:115
  75.3 25.9 %all-to-all-start.2 = ((bf16[4,2,4,32,512]{4,3,2,1,0:T(8,128)(2,1)}), bf16[4,2,4,32,512]{4,3,2,1,0:T(8,128)(2,1)S(1)}, u32[]{:S(2)}, u32[]{:S(2)}) async-start(bf16[4,2,4,32,512]{4,3,2,1,0:T(8,128)(2,1)} %broadcast_in_dim.196), calls=%async_computation.3 | async-start | bytes 2097152 | tf_op jit(solution)/shard_map/all_to_all | solution.py:113
  78.8 76.7 %reduce-scatter.5.cloned.1.call-start = ((), (), s32[]{:S(2)}) async-start(), calls=%async_computation.9 | async-start | bytes 1769472 | tf_op jit(solution)/shard_map/reduce_scatter | solution.py:145
  112.4 4.4 %collective-permute-start.8 = (bf16[512,1536]{1,0:T(8,128)(2,1)}, bf16[512,1536]{1,0:T(8,128)(2,1)}, u32[]{:S(2)}, u32[]{:S(2)}) collective-permute-start(bf16[512,1536]{1,0:T(8,128)(2,1)} %convolution_convert_fusion), channel_id=1, source_target_pairs={{0,1},{1,0},{2,3},{3,2},{4,5},{5,4},{6,7},{7,6},{8,9},{9,8},{10,11... | collective-permute-start | bytes 4718600 | tf_op jit(solution)/shard_map/ppermute | solution.py:146
  116.8 16.5 %all-to-all-start.3 = ((bf16[8,64,128]{2,1,0:T(8,128)(2,1)}), bf16[8,64,128]{2,1,0:T(8,128)(2,1)S(1)}, u32[]{:S(2)}, u32[]{:S(2)}) async-start(bf16[8,64,128]{2,1,0:T(8,128)(2,1)} %bitcast.47), calls=%async_computation.5 | async-start | bytes 262144 | tf_op jit(solution)/shard_map/all_to_all | solution.py:28
  127.9 18.6 %collective-permute-start.10 = (bf16[128,1536]{1,0:T(8,128)(2,1)S(1)}, bf16[128,1536]{1,0:T(8,128)(2,1)}, u32[]{:S(2)}, u32[]{:S(2)}) collective-permute-start(bf16[128,1536]{1,0:T(8,128)(2,1)S(1)} %get-tuple-element.70), channel_id=1, source_target_pairs={{0,4},{2,6},{4,0},{6,2},{1,5},{3,7},{5,1},{7,3},{8,12},{10,14},{12... | collective-permute-start | bytes 1179656 | tf_op jit(solution)/shard_map/ppermute | solution.py:17
  128.3 18.2 %collective-permute-start.11 = (bf16[128,1536]{1,0:T(8,128)(2,1)S(1)}, bf16[128,1536]{1,0:T(8,128)(2,1)}, u32[]{:S(2)}, u32[]{:S(2)}) collective-permute-start(bf16[128,1536]{1,0:T(8,128)(2,1)S(1)} %get-tuple-element.69), channel_id=1, source_target_pairs={{0,6},{2,0},{4,2},{6,4},{1,7},{3,1},{5,3},{7,5},{8,14},{10,8},{12,... | collective-permute-start | bytes 1179656 | tf_op jit(solution)/shard_map/ppermute | solution.py:17
  129.5 18.9 %collective-permute-start.9 = (bf16[128,1536]{1,0:T(8,128)(2,1)S(1)}, bf16[128,1536]{1,0:T(8,128)(2,1)}, u32[]{:S(2)}, u32[]{:S(2)}) collective-permute-start(bf16[128,1536]{1,0:T(8,128)(2,1)S(1)} %get-tuple-element.68), channel_id=1, source_target_pairs={{0,2},{2,4},{4,6},{6,0},{1,3},{3,5},{5,7},{7,1},{8,10},{10,12},{12... | collective-permute-start | bytes 1179656 | tf_op jit(solution)/shard_map/ppermute | solution.py:17
  133.4 5.7 %collective-permute-start.15 = (bf16[80,128]{1,0:T(8,128)(2,1)S(1)}, bf16[80,128]{1,0:T(8,128)(2,1)S(1)}, u32[]{:S(2)}, u32[]{:S(2)}) collective-permute-start(bf16[80,128]{1,0:T(8,128)(2,1)S(1)} %concatenate.32), channel_id=1, source_target_pairs={{64,0},{128,64},{192,128},{65,1},{129,65},{193,129},{66,2},{130,66... | collective-permute-start | bytes 61448 | tf_op jit(solution)/shard_map/ppermute | solution.py:44
  142.0 12.3 %all-to-all-start.4 = ((bf16[8,64,128]{2,1,0:T(8,128)(2,1)}), bf16[8,64,128]{2,1,0:T(8,128)(2,1)S(1)}, u32[]{:S(2)}, u32[]{:S(2)}) async-start(bf16[8,64,128]{2,1,0:T(8,128)(2,1)} %add_convert_fusion.1), calls=%async_computation.6 | async-start | bytes 262144 | tf_op jit(solution)/shard_map/all_to_all | solution.py:49
  157.1 6.9 %collective-permute-start.12 = (bf16[48,1536]{1,0:T(8,128)(2,1)}, bf16[48,1536]{1,0:T(8,128)(2,1)S(1)}, u32[]{:S(2)}, u32[]{:S(2)}) collective-permute-start(bf16[48,1536]{1,0:T(8,128)(2,1)} %get-tuple-element.73), channel_id=1, source_target_pairs={{0,192},{64,0},{128,64},{192,128},{1,193},{65,1},{129,65},{193,129... | collective-permute-start | bytes 442376 | tf_op jit(solution)/shard_map/ppermute | solution.py:17
  160.4 6.8 %collective-permute-start.13 = (bf16[48,1536]{1,0:T(8,128)(2,1)S(1)}, bf16[48,1536]{1,0:T(8,128)(2,1)S(1)}, u32[]{:S(2)}, u32[]{:S(2)}) collective-permute-start(bf16[48,1536]{1,0:T(8,128)(2,1)S(1)} %get-tuple-element.74), channel_id=1, source_target_pairs={{0,128},{64,192},{128,0},{192,64},{1,129},{65,193},{129,1},{193,65... | collective-permute-start | bytes 442376 | tf_op jit(solution)/shard_map/ppermute | solution.py:17
  160.9 7.8 %collective-permute-start.14 = (bf16[48,1536]{1,0:T(8,128)(2,1)S(1)}, bf16[48,1536]{1,0:T(8,128)(2,1)S(1)}, u32[]{:S(2)}, u32[]{:S(2)}) collective-permute-start(bf16[48,1536]{1,0:T(8,128)(2,1)S(1)} %get-tuple-element.71), channel_id=1, source_target_pairs={{0,64},{64,128},{128,192},{192,0},{1,65},{65,129},{129,193},{193,1... | collective-permute-start | bytes 442376 | tf_op jit(solution)/shard_map/ppermute | solution.py:17
  (23 other events, 116.9 us)
Sparse Core Ops, SparseCore 0:
  9.8 43.7 all-gather.1
  71.7 28.7 reduce-scatter.2
  115.4 39.6 reduce-scatter.4

commit v4 on v3

--- a/solution.py
+++ b/solution.py
@@ -67,14 +67,16 @@
     docs = doc_ids.astype(F32)
     first_doc, last_doc = docs[0], docs[-1]
     causal = jnp.tril(jnp.ones((tok, tok), dtype=bool))
-    allowed = (causal & (doc_ids[:, None] == doc_ids[None, :]))[None]
     in_first = (docs == first_doc)[:, None, None]
     in_last = (docs == last_doc)[:, None, None]
 
     pieces = out_grad.reshape(sub, ny, cols).transpose(1, 0, 2)
     key_last = jnp.where(in_last, key_heads, jnp.zeros_like(key_heads))
     local_state = jnp.einsum("thd,the->hde", key_last, value_heads, preferred_element_type=F32)
-    pieces, local_state = lax.optimization_barrier((pieces, local_state.astype(BF)))
+    pieces, local_state, block_docs = lax.optimization_barrier(
+        (pieces, local_state.astype(BF), doc_ids)
+    )
+    allowed = (causal & (block_docs[:, None] == block_docs[None, :]))[None]
     row, place = lax.axis_index("y"), lax.axis_index("x")
     piece = [lax.dynamic_index_in_dim(pieces, row, 0, False)]
     for step in range(1, ny):
@@ -157,6 +159,7 @@
     last = jnp.concatenate(
         [out_sum, wg_sum.reshape(ny, rows, cols)], axis=1
     )
+    future, last = lax.optimization_barrier((future, last))
     blocks = [None] * ny
     for step in range(ny):
         block = lax.dynamic_index_in_dim(last, (row + step) % ny, 0, False)

time: 178 us -> 179 us (level)
  local copies, waits for them, and re-layouts: 21.5 us -> 27.1 us
  waiting for transfers between devices: 51.3 us -> 46.6 us
    ppermute x12, waiting for transfers between devices: 13.4 us -> 8.48 us  [turn(): return lax.ppermute(x, axis, [(i, (i + by) % count) for i in range(count)])]
    unnamed x59 -> x54, local copies, waits for them, and re-layouts: 6.19 us -> 8.55 us
    all_to_all x2, waiting for transfers between devices: 5.77 us -> 3.58 us  [row_state(): out = lax.all_to_all(total, 'z', 0, 0)]
  transfers between devices with their start and end apart: 24 -> 24, of which waited for: 13 -> 12; matrix products, arithmetic and copies ran while one was open for 21% -> 24% of each run, Pallas kernels for 0% -> 0%
where the time goes in v4:
time: 179 us; the launch traced here: 177 us
  starting transfers between devices  50.4 us (28%)
  waiting for transfers between devices  46.6 us (26%)
  local copies, waits for them, and re-layouts  27.1 us (15%)
  matrix products  20.6 us (12%)
  between operations  18.5 us (10%)
  other arithmetic  13.9 us (8%)
    all_to_all x1, waiting for transfers between devices, shards(): normed_all = lax.all_to_all(by_core, 'y', 0, 0).transpose(1, 2, 0, 3, 4)  21.6 us
    all_to_all x2, starting transfers between devices, row_state(): got = lax.all_to_all(slices, 'z', 0, 0)  15.4 us
    ppermute x12, starting transfers between devices, turn(): return lax.ppermute(x, axis, [(i, (i + by) % count) for i in range(count)])  14.7 us
    all_to_all x2, starting transfers between devices, row_state(): out = lax.all_to_all(total, 'z', 0, 0)  11.4 us
    unnamed x54, local copies, waits for them, and re-layouts  8.55 us
    ppermute x12, waiting for transfers between devices, turn(): return lax.ppermute(x, axis, [(i, (i + by) % count) for i in range(count)])  8.48 us
    dot_general x2, matrix products, project(): lax.dot_general(rows, weight_t, (((1,), (1,)), ((), ())), preferred_eleme...  6.58 us
    all_to_all x2, waiting for transfers between devices, row_state(): got = lax.all_to_all(slices, 'z', 0, 0)  6.31 us
  transfers between devices with their start and end apart: 24, of which 12 were waited for; matrix products, arithmetic and copies ran while one was open for 24% of the time, Pallas kernels for 0%

profile of v4, /device:TPU:32, one launch (start us, length us, event | category | flops | bytes accessed | tf_op | source)
XLA Modules:
  0.0 177.2 jit_solution(9486238645104704088)
XLA Ops:
  13.7 3.1 %collective-permute-start.1 = (bf16[32,1536]{1,0:T(8,128)(2,1)S(1)}, bf16[32,1536]{1,0:T(8,128)(2,1)S(1)}, u32[]{:S(2)}, u32[]{:S(2)}) collective-permute-start(bf16[32,1536]{1,0:T(8,128)(2,1)S(1)} %bitcast.213), channel_id=1, source_target_pairs={{0,192},{64,0},{128,64},{192,128},{1,193},{65,1},{129,65},{193,129... | collective-permute-start | bytes 294920 | tf_op jit(solution)/shard_map/ppermute | solution.py:17
  20.8 8.6 %all-to-all-start = ((bf16[8,80,128]{2,1,0:T(8,128)(2,1)}), bf16[8,80,128]{2,1,0:T(8,128)(2,1)S(1)}, u32[]{:S(2)}, u32[]{:S(2)}) async-start(bf16[8,80,128]{2,1,0:T(8,128)(2,1)} %pad_maximum_fusion.4), calls=%async_computation | async-start | bytes 327680 | tf_op jit(solution)/shard_map/all_to_all | solution.py:28
  29.9 2.6 %stack.61 = bf16[8,32,1536]{2,0,1:T(8,128)(2,1)S(1)} concatenate(bf16[1,32,1536]{2,0,1:T(2,128)(2,1)S(1)} %get-tuple-element.84, bf16[1,32,1536]{2,0,1:T(2,128)(2,1)S(1)} %copy.168, bf16[1,32,1536]{2,0,1:T(2,128)(2,1)S(1)} %copy.169, bf16[1,32,1536]{2,0,1:T(2,128)(2,1)S(1)} %copy.170, bf16[1,32,1536]{2,0,1:T(2,128)(2,1)S(1)} %get-tuple-element.84, ...), dimensions={0} | concatenate | bytes 1572864 | tf_op jit(solution)/shard_map/stack | solution.py:85
  32.7 2.8 %collective-permute-start.4 = (bf16[4,32,1536]{2,0,1:T(4,128)(2,1)S(1)}, bf16[4,32,1536]{2,0,1:T(4,128)(2,1)S(1)}, u32[]{:S(2)}, u32[]{:S(2)}) collective-permute-start(bf16[4,32,1536]{2,0,1:T(4,128)(2,1)S(1)} %constant_dynamic-slice_fusion.1), channel_id=1, source_target_pairs={{0,6},{2,0},{4,2},{6,4},{1,7},{3,1},{5,3},{7,5},{8,14},{10,8},{12,... | collective-permute-start | bytes 1179656 | tf_op jit(solution)/shard_map/ppermute | solution.py:17
  37.2 2.3 %all-to-all-done = bf16[8,80,128]{2,1,0:T(8,128)(2,1)S(1)} async-done(((bf16[8,80,128]{2,1,0:T(8,128)(2,1)}), bf16[8,80,128]{2,1,0:T(8,128)(2,1)S(1)}, u32[]{:S(2)}, u32[]{:S(2)}) %all-to-all-start) | async-done | bytes 163872 | tf_op jit(solution)/shard_map/all_to_all | solution.py:28
  41.3 2.1 %compare_reduce_fusion.1 = (pred[8]{0:T(512)(128)(4,1)}, pred[8]{0:T(512)(128)(4,1)S(1)}) fusion(f32[]{:T(128)} %bitcast.35, bf16[8,80,128]{2,1,0:T(8,128)(2,1)S(1)} %all-to-all-done, f32[]{:T(128)} %bitcast.5), kind=kLoop, calls=%fused_computation.102 | loop fusion | flops 32 | bytes 56 | tf_op jit(solution)/shard_map/eq | solution.py:42
  43.6 3.9 %collective-permute-start = (bf16[80,128]{1,0:T(8,128)(2,1)S(1)}, bf16[80,128]{1,0:T(8,128)(2,1)S(1)}, u32[]{:S(2)}, u32[]{:S(2)}) collective-permute-start(bf16[80,128]{1,0:T(8,128)(2,1)S(1)} %concatenate.27), channel_id=1, source_target_pairs={{0,64},{64,128},{128,192},{1,65},{65,129},{129,193},{2,66},{66,130... | collective-permute-start | bytes 61448 | tf_op jit(solution)/shard_map/ppermute | solution.py:44
  51.1 3.5 %collective-permute-done.6 = bf16[4,32,1536]{2,0,1:T(4,128)(2,1)S(1)} collective-permute-done((bf16[4,32,1536]{2,0,1:T(4,128)(2,1)S(1)}, bf16[4,32,1536]{2,0,1:T(4,128)(2,1)S(1)}, u32[]{:S(2)}, u32[]{:S(2)}) %collective-permute-start.6) | collective-permute-done | bytes 393248 | tf_op jit(solution)/shard_map/ppermute | solution.py:17
  58.2 7.2 %all-to-all-start.1 = ((bf16[8,64,128]{2,1,0:T(8,128)(2,1)}), bf16[8,64,128]{2,1,0:T(8,128)(2,1)S(1)}, u32[]{:S(2)}, u32[]{:S(2)}) async-start(bf16[8,64,128]{2,1,0:T(8,128)(2,1)} %add_convert_fusion.2), calls=%async_computation.2 | async-start | bytes 262144 | tf_op jit(solution)/shard_map/all_to_all | solution.py:49
  65.5 2.5 %convolution_convert_fusion.2 = bf16[512,512]{1,0:T(8,128)(2,1)S(1)} fusion(bf16[512,1536]{1,0:T(8,128)(2,1)S(1)} %bitcast.176, bf16[1536,512]{1,0:T(8,128)(2,1)} %all-gather.2.cloned.1.call-done), kind=kOutput, calls=%fused_computation.12 | convolution fusion | flops 805568512 | bytes 3670016 | tf_op jit(solution)/shard_map/dot_general | solution.py:96
  68.0 2.4 %convolution_convert_fusion.1 = bf16[512,512]{1,0:T(8,128)(2,1)S(1)} fusion(bf16[512,1536]{1,0:T(8,128)(2,1)} %collective-permute-done.7, bf16[1536,512]{1,0:T(8,128)(2,1)S(1)} %copy-done.19), kind=kOutput, calls=%fused_computation.11 | convolution fusion | flops 805568512 | bytes 3670016 | tf_op jit(solution)/shard_map/dot_general | solution.py:96
  75.2 3.5 %all-to-all-start.2 = ((bf16[4,2,4,32,512]{4,3,2,1,0:T(8,128)(2,1)}), bf16[4,2,4,32,512]{4,3,2,1,0:T(8,128)(2,1)S(1)}, u32[]{:S(2)}, u32[]{:S(2)}) async-start(bf16[4,2,4,32,512]{4,3,2,1,0:T(8,128)(2,1)} %broadcast_in_dim.197), calls=%async_computation.3 | async-start | bytes 2097152 | tf_op jit(solution)/shard_map/all_to_all | solution.py:115
  79.6 21.6 %all-to-all-done.2 = bf16[4,2,4,32,512]{4,3,2,1,0:T(8,128)(2,1)S(1)} async-done(((bf16[4,2,4,32,512]{4,3,2,1,0:T(8,128)(2,1)}), bf16[4,2,4,32,512]{4,3,2,1,0:T(8,128)(2,1)S(1)}, u32[]{:S(2)}, u32[]{:S(2)}) %all-to-all-start.2) | async-done | bytes 1048608 | tf_op jit(solution)/shard_map/all_to_all | solution.py:115
  102.2 2.1 %fusion.18 = f32[512,1536]{1,0:T(8,128)S(1)} fusion(bf16[512,1536]{1,0:T(8,128)(2,1)S(1)} %bitcast.177, bf16[2,512,512]{2,1,0:T(8,128)(2,1)} %bitcast.180), kind=kOutput, calls=%fused_computation.44 | convolution fusion | flops 805306368 | bytes 5242880 | tf_op jit(solution)/shard_map/dot_general | solution.py:127
  104.3 2.4 %fusion = bf16[512,1536]{1,0:T(8,128)(2,1)S(1)} fusion(f32[512,1536]{1,0:T(8,128)S(1)} %fusion.18, bf16[512,1536]{1,0:T(8,128)(2,1)} %collective-permute-done.7, bf16[2,512,512]{2,1,0:T(8,128)(2,1)S(1)} %bitcast.181), kind=kOutput, calls=%fused_computation.3 | convolution fusion | flops 806879232 | bytes 6815744 | tf_op jit(solution)/shard_map/dot_general | solution.py:129
  108.0 3.6 %convolution_convert_fusion = bf16[512,1536]{1,0:T(8,128)(2,1)} fusion(bf16[1536,512]{1,0:T(8,128)(2,1)} %all-gather.2.cloned.1.call-done, bf16[2,512,512]{2,1,0:T(8,128)(2,1)S(1)} %bitcast.182), kind=kOutput, calls=%fused_computation.2 | convolution fusion | flops 806092800 | bytes 3670016 | tf_op jit(solution)/shard_map/dot_general | solution.py:123
  117.1 6.9 %all-to-all-start.3 = ((bf16[8,64,128]{2,1,0:T(8,128)(2,1)}), bf16[8,64,128]{2,1,0:T(8,128)(2,1)S(1)}, u32[]{:S(2)}, u32[]{:S(2)}) async-start(bf16[8,64,128]{2,1,0:T(8,128)(2,1)} %bitcast.212), calls=%async_computation.4 | async-start | bytes 262144 | tf_op jit(solution)/shard_map/all_to_all | solution.py:28
  124.0 2.9 %fusion.1 = bf16[512,1536]{1,0:T(8,128)(2,1)S(1)} fusion(bf16[512,1536]{1,0:T(8,128)(2,1)} %collective-permute-done.8, bf16[1536,512]{1,0:T(8,128)(2,1)} %all-gather.2.cloned.1.call-done, bf16[2,512,512]{2,1,0:T(8,128)(2,1)S(1)} %bitcast.183), kind=kOutput, calls=%fused_computation.4 | convolution fusion | flops 807665664 | bytes 5242880 | tf_op jit(solution)/shard_map/dot_general | solution.py:123
  129.8 4.0 %all-to-all-done.3 = bf16[8,64,128]{2,1,0:T(8,128)(2,1)S(1)} async-done(((bf16[8,64,128]{2,1,0:T(8,128)(2,1)}), bf16[8,64,128]{2,1,0:T(8,128)(2,1)S(1)}, u32[]{:S(2)}, u32[]{:S(2)}) %all-to-all-start.3) | async-done | bytes 131104 | tf_op jit(solution)/shard_map/all_to_all | solution.py:28
  135.5 4.1 %collective-permute-done.9 = bf16[80,128]{1,0:T(8,128)(2,1)S(1)} collective-permute-done((bf16[80,128]{1,0:T(8,128)(2,1)S(1)}, bf16[80,128]{1,0:T(8,128)(2,1)S(1)}, u32[]{:S(2)}, u32[]{:S(2)}) %collective-permute-start.9) | collective-permute-done | bytes 20512 | tf_op jit(solution)/shard_map/ppermute | solution.py:44
  142.5 4.2 %all-to-all-start.4 = ((bf16[8,64,128]{2,1,0:T(8,128)(2,1)}), bf16[8,64,128]{2,1,0:T(8,128)(2,1)S(1)}, u32[]{:S(2)}, u32[]{:S(2)}) async-start(bf16[8,64,128]{2,1,0:T(8,128)(2,1)} %add_convert_fusion.1), calls=%async_computation.5 | async-start | bytes 262144 | tf_op jit(solution)/shard_map/all_to_all | solution.py:49
  146.6 2.1 %collective-permute-done.10 = bf16[128,1536]{1,0:T(8,128)(2,1)} collective-permute-done((bf16[128,1536]{1,0:T(8,128)(2,1)S(1)}, bf16[128,1536]{1,0:T(8,128)(2,1)}, u32[]{:S(2)}, u32[]{:S(2)}) %collective-permute-start.10) | collective-permute-done | bytes 393248 | tf_op jit(solution)/shard_map/ppermute | solution.py:17
  152.2 2.2 %all-to-all-done.4 = bf16[8,64,128]{2,1,0:T(8,128)(2,1)S(1)} async-done(((bf16[8,64,128]{2,1,0:T(8,128)(2,1)}), bf16[8,64,128]{2,1,0:T(8,128)(2,1)S(1)}, u32[]{:S(2)}, u32[]{:S(2)}) %all-to-all-start.4) | async-done | bytes 131104 | tf_op jit(solution)/shard_map/all_to_all | solution.py:49
  155.3 3.0 %collective-permute-start.14 = (bf16[48,1536]{1,0:T(8,128)(2,1)S(1)}, bf16[48,1536]{1,0:T(8,128)(2,1)S(1)}, u32[]{:S(2)}, u32[]{:S(2)}) collective-permute-start(bf16[48,1536]{1,0:T(8,128)(2,1)S(1)} %get-tuple-element.79), channel_id=1, source_target_pairs={{0,128},{64,192},{128,0},{192,64},{1,129},{65,193},{129,1},{193,65... | collective-permute-start | bytes 442376 | tf_op jit(solution)/shard_map/ppermute | solution.py:17
  (167 shorter events, 55.0 us)
Async XLA Ops:
  7.2 47.4 %all-gather.2.cloned.1.call-start = ((), (), s32[]{:S(2)}) async-start(), calls=%async_computation.7 | async-start | bytes 1769472 | tf_op jit(solution)/shard_map/all_gather | solution.py:63
  13.7 15.6 %collective-permute-start.1 = (bf16[32,1536]{1,0:T(8,128)(2,1)S(1)}, bf16[32,1536]{1,0:T(8,128)(2,1)S(1)}, u32[]{:S(2)}, u32[]{:S(2)}) collective-permute-start(bf16[32,1536]{1,0:T(8,128)(2,1)S(1)} %bitcast.213), channel_id=1, source_target_pairs={{0,192},{64,0},{128,64},{192,128},{1,193},{65,1},{129,65},{193,129... | collective-permute-start | bytes 294920 | tf_op jit(solution)/shard_map/ppermute | solution.py:17
  16.9 12.7 %collective-permute-start.2 = (bf16[32,1536]{1,0:T(8,128)(2,1)S(1)}, bf16[32,1536]{1,0:T(8,128)(2,1)S(1)}, u32[]{:S(2)}, u32[]{:S(2)}) collective-permute-start(bf16[32,1536]{1,0:T(8,128)(2,1)S(1)} %bitcast.215), channel_id=1, source_target_pairs={{0,128},{64,192},{128,0},{192,64},{1,129},{65,193},{129,1},{193,65... | collective-permute-start | bytes 294920 | tf_op jit(solution)/shard_map/ppermute | solution.py:17
  17.6 12.1 %collective-permute-start.3 = (bf16[32,1536]{1,0:T(8,128)(2,1)S(1)}, bf16[32,1536]{1,0:T(8,128)(2,1)S(1)}, u32[]{:S(2)}, u32[]{:S(2)}) collective-permute-start(bf16[32,1536]{1,0:T(8,128)(2,1)S(1)} %bitcast.217), channel_id=1, source_target_pairs={{0,64},{64,128},{128,192},{192,0},{1,65},{65,129},{129,193},{193,1... | collective-permute-start | bytes 294920 | tf_op jit(solution)/shard_map/ppermute | solution.py:17
  20.8 18.7 %all-to-all-start = ((bf16[8,80,128]{2,1,0:T(8,128)(2,1)}), bf16[8,80,128]{2,1,0:T(8,128)(2,1)S(1)}, u32[]{:S(2)}, u32[]{:S(2)}) async-start(bf16[8,80,128]{2,1,0:T(8,128)(2,1)} %pad_maximum_fusion.4), calls=%async_computation | async-start | bytes 327680 | tf_op jit(solution)/shard_map/all_to_all | solution.py:28
  32.7 18.4 %collective-permute-start.4 = (bf16[4,32,1536]{2,0,1:T(4,128)(2,1)S(1)}, bf16[4,32,1536]{2,0,1:T(4,128)(2,1)S(1)}, u32[]{:S(2)}, u32[]{:S(2)}) collective-permute-start(bf16[4,32,1536]{2,0,1:T(4,128)(2,1)S(1)} %constant_dynamic-slice_fusion.1), channel_id=1, source_target_pairs={{0,6},{2,0},{4,2},{6,4},{1,7},{3,1},{5,3},{7,5},{8,14},{10,8},{12,... | collective-permute-start | bytes 1179656 | tf_op jit(solution)/shard_map/ppermute | solution.py:17
  35.5 15.6 %collective-permute-start.5 = (bf16[4,32,1536]{2,0,1:T(4,128)(2,1)S(1)}, bf16[4,32,1536]{2,0,1:T(4,128)(2,1)S(1)}, u32[]{:S(2)}, u32[]{:S(2)}) collective-permute-start(bf16[4,32,1536]{2,0,1:T(4,128)(2,1)S(1)} %constant_dynamic-slice_fusion.1), channel_id=1, source_target_pairs={{0,4},{2,6},{4,0},{6,2},{1,5},{3,7},{5,1},{7,3},{8,12},{10,14},{12... | collective-permute-start | bytes 1179656 | tf_op jit(solution)/shard_map/ppermute | solution.py:17
  36.3 18.3 %collective-permute-start.6 = (bf16[4,32,1536]{2,0,1:T(4,128)(2,1)S(1)}, bf16[4,32,1536]{2,0,1:T(4,128)(2,1)S(1)}, u32[]{:S(2)}, u32[]{:S(2)}) collective-permute-start(bf16[4,32,1536]{2,0,1:T(4,128)(2,1)S(1)} %constant_dynamic-slice_fusion.1), channel_id=1, source_target_pairs={{0,2},{2,4},{4,6},{6,0},{1,3},{3,5},{5,7},{7,1},{8,10},{10,12},{12... | collective-permute-start | bytes 1179656 | tf_op jit(solution)/shard_map/ppermute | solution.py:17
  43.6 5.4 %collective-permute-start = (bf16[80,128]{1,0:T(8,128)(2,1)S(1)}, bf16[80,128]{1,0:T(8,128)(2,1)S(1)}, u32[]{:S(2)}, u32[]{:S(2)}) collective-permute-start(bf16[80,128]{1,0:T(8,128)(2,1)S(1)} %concatenate.27), channel_id=1, source_target_pairs={{0,64},{64,128},{128,192},{1,65},{65,129},{129,193},{2,66},{66,130... | collective-permute-start | bytes 61448 | tf_op jit(solution)/shard_map/ppermute | solution.py:44
  56.4 11.6 %collective-permute-start.7 = (bf16[512,1536]{1,0:T(8,128)(2,1)S(1)}, bf16[512,1536]{1,0:T(8,128)(2,1)}, u32[]{:S(2)}, u32[]{:S(2)}) collective-permute-start(bf16[512,1536]{1,0:T(8,128)(2,1)S(1)} %bitcast.175), channel_id=1, source_target_pairs={{0,1},{1,0},{2,3},{3,2},{4,5},{5,4},{6,7},{7,6},{8,9},{9,8},{10,11... | collective-permute-start | bytes 4718600 | tf_op jit(solution)/shard_map/ppermute | solution.py:94
  58.2 15.0 %all-to-all-start.1 = ((bf16[8,64,128]{2,1,0:T(8,128)(2,1)}), bf16[8,64,128]{2,1,0:T(8,128)(2,1)S(1)}, u32[]{:S(2)}, u32[]{:S(2)}) async-start(bf16[8,64,128]{2,1,0:T(8,128)(2,1)} %add_convert_fusion.2), calls=%async_computation.2 | async-start | bytes 262144 | tf_op jit(solution)/shard_map/all_to_all | solution.py:49
  65.5 36.7 %reduce-scatter.3.cloned.1.call-start = ((), (), s32[]{:S(2)}) async-start(), calls=%async_computation.8 | async-start | bytes 1310720 | tf_op jit(solution)/shard_map/reduce_scatter | solution.py:117
  75.2 25.9 %all-to-all-start.2 = ((bf16[4,2,4,32,512]{4,3,2,1,0:T(8,128)(2,1)}), bf16[4,2,4,32,512]{4,3,2,1,0:T(8,128)(2,1)S(1)}, u32[]{:S(2)}, u32[]{:S(2)}) async-start(bf16[4,2,4,32,512]{4,3,2,1,0:T(8,128)(2,1)} %broadcast_in_dim.197), calls=%async_computation.3 | async-start | bytes 2097152 | tf_op jit(solution)/shard_map/all_to_all | solution.py:115
  78.8 72.4 %reduce-scatter.5.cloned.1.call-start = ((), (), s32[]{:S(2)}) async-start(), calls=%async_computation.9 | async-start | bytes 1769472 | tf_op jit(solution)/shard_map/reduce_scatter | solution.py:147
  111.7 5.4 %collective-permute-start.8 = (bf16[512,1536]{1,0:T(8,128)(2,1)}, bf16[512,1536]{1,0:T(8,128)(2,1)}, u32[]{:S(2)}, u32[]{:S(2)}) collective-permute-start(bf16[512,1536]{1,0:T(8,128)(2,1)} %convolution_convert_fusion), channel_id=1, source_target_pairs={{0,1},{1,0},{2,3},{3,2},{4,5},{5,4},{6,7},{7,6},{8,9},{9,8},{10,11... | collective-permute-start | bytes 4718600 | tf_op jit(solution)/shard_map/ppermute | solution.py:148
  117.1 16.7 %all-to-all-start.3 = ((bf16[8,64,128]{2,1,0:T(8,128)(2,1)}), bf16[8,64,128]{2,1,0:T(8,128)(2,1)S(1)}, u32[]{:S(2)}, u32[]{:S(2)}) async-start(bf16[8,64,128]{2,1,0:T(8,128)(2,1)} %bitcast.212), calls=%async_computation.4 | async-start | bytes 262144 | tf_op jit(solution)/shard_map/all_to_all | solution.py:28
  127.8 18.9 %collective-permute-start.12 = (bf16[128,1536]{1,0:T(8,128)(2,1)}, bf16[128,1536]{1,0:T(8,128)(2,1)}, u32[]{:S(2)}, u32[]{:S(2)}) collective-permute-start(bf16[128,1536]{1,0:T(8,128)(2,1)} %get-tuple-element.75), channel_id=1, source_target_pairs={{0,6},{2,0},{4,2},{6,4},{1,7},{3,1},{5,3},{7,5},{8,14},{10,8},{12,... | collective-permute-start | bytes 1179656 | tf_op jit(solution)/shard_map/ppermute | solution.py:17
  128.0 18.6 %collective-permute-start.11 = (bf16[128,1536]{1,0:T(8,128)(2,1)S(1)}, bf16[128,1536]{1,0:T(8,128)(2,1)}, u32[]{:S(2)}, u32[]{:S(2)}) collective-permute-start(bf16[128,1536]{1,0:T(8,128)(2,1)S(1)} %get-tuple-element.76), channel_id=1, source_target_pairs={{0,4},{2,6},{4,0},{6,2},{1,5},{3,7},{5,1},{7,3},{8,12},{10,14},{12... | collective-permute-start | bytes 1179656 | tf_op jit(solution)/shard_map/ppermute | solution.py:17
  128.8 20.0 %collective-permute-start.10 = (bf16[128,1536]{1,0:T(8,128)(2,1)S(1)}, bf16[128,1536]{1,0:T(8,128)(2,1)}, u32[]{:S(2)}, u32[]{:S(2)}) collective-permute-start(bf16[128,1536]{1,0:T(8,128)(2,1)S(1)} %get-tuple-element.74), channel_id=1, source_target_pairs={{0,2},{2,4},{4,6},{6,0},{1,3},{3,5},{5,7},{7,1},{8,10},{10,12},{12... | collective-permute-start | bytes 1179656 | tf_op jit(solution)/shard_map/ppermute | solution.py:17
  133.9 5.7 %collective-permute-start.9 = (bf16[80,128]{1,0:T(8,128)(2,1)S(1)}, bf16[80,128]{1,0:T(8,128)(2,1)S(1)}, u32[]{:S(2)}, u32[]{:S(2)}) collective-permute-start(bf16[80,128]{1,0:T(8,128)(2,1)S(1)} %concatenate.31), channel_id=1, source_target_pairs={{64,0},{128,64},{192,128},{65,1},{129,65},{193,129},{66,2},{130,66... | collective-permute-start | bytes 61448 | tf_op jit(solution)/shard_map/ppermute | solution.py:44
  142.5 11.8 %all-to-all-start.4 = ((bf16[8,64,128]{2,1,0:T(8,128)(2,1)}), bf16[8,64,128]{2,1,0:T(8,128)(2,1)S(1)}, u32[]{:S(2)}, u32[]{:S(2)}) async-start(bf16[8,64,128]{2,1,0:T(8,128)(2,1)} %add_convert_fusion.1), calls=%async_computation.5 | async-start | bytes 262144 | tf_op jit(solution)/shard_map/all_to_all | solution.py:49
  155.0 5.5 %collective-permute-start.13 = (bf16[48,1536]{1,0:T(8,128)(2,1)S(1)}, bf16[48,1536]{1,0:T(8,128)(2,1)S(1)}, u32[]{:S(2)}, u32[]{:S(2)}) collective-permute-start(bf16[48,1536]{1,0:T(8,128)(2,1)S(1)} %get-tuple-element.80), channel_id=1, source_target_pairs={{0,192},{64,0},{128,64},{192,128},{1,193},{65,1},{129,65},{193,129... | collective-permute-start | bytes 442376 | tf_op jit(solution)/shard_map/ppermute | solution.py:17
  155.3 7.2 %collective-permute-start.14 = (bf16[48,1536]{1,0:T(8,128)(2,1)S(1)}, bf16[48,1536]{1,0:T(8,128)(2,1)S(1)}, u32[]{:S(2)}, u32[]{:S(2)}) collective-permute-start(bf16[48,1536]{1,0:T(8,128)(2,1)S(1)} %get-tuple-element.79), channel_id=1, source_target_pairs={{0,128},{64,192},{128,0},{192,64},{1,129},{65,193},{129,1},{193,65... | collective-permute-start | bytes 442376 | tf_op jit(solution)/shard_map/ppermute | solution.py:17
  158.3 6.4 %collective-permute-start.15 = (bf16[48,1536]{1,0:T(8,128)(2,1)S(1)}, bf16[48,1536]{1,0:T(8,128)(2,1)S(1)}, u32[]{:S(2)}, u32[]{:S(2)}) collective-permute-start(bf16[48,1536]{1,0:T(8,128)(2,1)S(1)} %get-tuple-element.77), channel_id=1, source_target_pairs={{0,64},{64,128},{128,192},{192,0},{1,65},{65,129},{129,193},{193,1... | collective-permute-start | bytes 442376 | tf_op jit(solution)/shard_map/ppermute | solution.py:17
  (20 other events, 101.2 us)
Sparse Core Ops, SparseCore 0:
  9.8 43.7 all-gather.1
  71.7 28.6 reduce-scatter.2
  112.6 38.5 reduce-scatter.4

commit v5 on v4

--- a/solution.py
+++ b/solution.py
@@ -164,8 +164,8 @@
     for step in range(ny):
         block = lax.dynamic_index_in_dim(last, (row + step) % ny, 0, False)
         blocks[-step] = turn(block, "y", step) if step else block
-    last = lax.dynamic_slice_in_dim(jnp.stack(blocks + blocks), (ny - row) % ny, ny, 0)
-    last = last.transpose(1, 0, 2).reshape(sub + rows, ny * cols)
+    last = [lax.select_n((slot - row) % ny, *blocks) for slot in range(ny)]
+    last = jnp.concatenate(last, axis=1)
     layer_out, weight_grad = last[:sub], last[sub:]
 
     future = future.reshape(heads, HD, HD)

time: 179 us -> 174 us (0.972)
  local copies, waits for them, and re-layouts: 27.1 us -> 20.9 us
    unnamed x54 -> x50, local copies, waits for them, and re-layouts: 8.55 us -> 5.2 us
    ppermute x12, waiting for transfers between devices: 8.48 us -> 10.3 us  [turn(): return lax.ppermute(x, axis, [(i, (i + by) % count) for i in range(count)])]
where the time goes in v5:
time: 174 us; the launch traced here: 171 us
  starting transfers between devices  50.4 us (29%)
  waiting for transfers between devices  47.6 us (27%)
  local copies, waits for them, and re-layouts  20.9 us (12%)
  matrix products  19.2 us (11%)
  between operations  18.6 us (11%)
  other arithmetic  14.8 us (9%)
    all_to_all x1, waiting for transfers between devices, shards(): normed_all = lax.all_to_all(by_core, 'y', 0, 0).transpose(1, 2, 0, 3, 4)  21.5 us
    all_to_all x2, starting transfers between devices, row_state(): got = lax.all_to_all(slices, 'z', 0, 0)  15.4 us
    ppermute x12, starting transfers between devices, turn(): return lax.ppermute(x, axis, [(i, (i + by) % count) for i in range(count)])  14.8 us
    all_to_all x2, starting transfers between devices, row_state(): out = lax.all_to_all(total, 'z', 0, 0)  11.4 us
    ppermute x12, waiting for transfers between devices, turn(): return lax.ppermute(x, axis, [(i, (i + by) % count) for i in range(count)])  10.3 us
    all_to_all x2, waiting for transfers between devices, row_state(): got = lax.all_to_all(slices, 'z', 0, 0)  6.09 us
    unnamed x50, local copies, waits for them, and re-layouts  5.2 us
    ppermute x2, starting transfers between devices, row_state(): message = lax.ppermute(message, 'y', pairs)  5.19 us
  transfers between devices with their start and end apart: 24, of which 12 were waited for; matrix products, arithmetic and copies ran while one was open for 24% of the time, Pallas kernels for 0%

profile of v5, /device:TPU:32, one launch (start us, length us, event | category | flops | bytes accessed | tf_op | source)
XLA Modules:
  0.0 171.5 jit_solution(8808851632461831176)
XLA Ops:
  13.7 3.1 %collective-permute-start.1 = (bf16[32,1536]{1,0:T(8,128)(2,1)S(1)}, bf16[32,1536]{1,0:T(8,128)(2,1)S(1)}, u32[]{:S(2)}, u32[]{:S(2)}) collective-permute-start(bf16[32,1536]{1,0:T(8,128)(2,1)S(1)} %bitcast.206), channel_id=1, source_target_pairs={{0,192},{64,0},{128,64},{192,128},{1,193},{65,1},{129,65},{193,129... | collective-permute-start | bytes 294920 | tf_op jit(solution)/shard_map/ppermute | solution.py:17
  20.8 8.6 %all-to-all-start = ((bf16[8,80,128]{2,1,0:T(8,128)(2,1)}), bf16[8,80,128]{2,1,0:T(8,128)(2,1)S(1)}, u32[]{:S(2)}, u32[]{:S(2)}) async-start(bf16[8,80,128]{2,1,0:T(8,128)(2,1)} %pad_maximum_fusion.6), calls=%async_computation | async-start | bytes 327680 | tf_op jit(solution)/shard_map/all_to_all | solution.py:28
  29.9 2.6 %stack.44 = bf16[8,32,1536]{2,0,1:T(8,128)(2,1)S(1)} concatenate(bf16[1,32,1536]{2,0,1:T(2,128)(2,1)S(1)} %get-tuple-element.87, bf16[1,32,1536]{2,0,1:T(2,128)(2,1)S(1)} %copy.160, bf16[1,32,1536]{2,0,1:T(2,128)(2,1)S(1)} %copy.161, bf16[1,32,1536]{2,0,1:T(2,128)(2,1)S(1)} %copy.162, bf16[1,32,1536]{2,0,1:T(2,128)(2,1)S(1)} %get-tuple-element.87, ...), dimensions={0} | concatenate | bytes 1572864 | tf_op jit(solution)/shard_map/stack | solution.py:85
  32.7 2.8 %collective-permute-start.4 = (bf16[4,32,1536]{2,0,1:T(4,128)(2,1)S(1)}, bf16[4,32,1536]{2,0,1:T(4,128)(2,1)S(1)}, u32[]{:S(2)}, u32[]{:S(2)}) collective-permute-start(bf16[4,32,1536]{2,0,1:T(4,128)(2,1)S(1)} %constant_dynamic-slice_fusion.1), channel_id=1, source_target_pairs={{0,6},{2,0},{4,2},{6,4},{1,7},{3,1},{5,3},{7,5},{8,14},{10,8},{12,... | collective-permute-start | bytes 1179656 | tf_op jit(solution)/shard_map/ppermute | solution.py:17
  37.2 2.3 %all-to-all-done = bf16[8,80,128]{2,1,0:T(8,128)(2,1)S(1)} async-done(((bf16[8,80,128]{2,1,0:T(8,128)(2,1)}), bf16[8,80,128]{2,1,0:T(8,128)(2,1)S(1)}, u32[]{:S(2)}, u32[]{:S(2)}) %all-to-all-start) | async-done | bytes 163872 | tf_op jit(solution)/shard_map/all_to_all | solution.py:28
  41.3 2.1 %compare_reduce_fusion.1 = (pred[8]{0:T(512)(128)(4,1)}, pred[8]{0:T(512)(128)(4,1)S(1)}) fusion(f32[]{:T(128)} %bitcast.35, bf16[8,80,128]{2,1,0:T(8,128)(2,1)S(1)} %all-to-all-done, f32[]{:T(128)} %bitcast.5), kind=kLoop, calls=%fused_computation.101 | loop fusion | flops 32 | bytes 56 | tf_op jit(solution)/shard_map/eq | solution.py:42
  43.5 3.9 %collective-permute-start = (bf16[80,128]{1,0:T(8,128)(2,1)S(1)}, bf16[80,128]{1,0:T(8,128)(2,1)S(1)}, u32[]{:S(2)}, u32[]{:S(2)}) collective-permute-start(bf16[80,128]{1,0:T(8,128)(2,1)S(1)} %concatenate.30), channel_id=1, source_target_pairs={{0,64},{64,128},{128,192},{1,65},{65,129},{129,193},{2,66},{66,130... | collective-permute-start | bytes 61448 | tf_op jit(solution)/shard_map/ppermute | solution.py:44
  51.0 3.6 %collective-permute-done.6 = bf16[4,32,1536]{2,0,1:T(4,128)(2,1)S(1)} collective-permute-done((bf16[4,32,1536]{2,0,1:T(4,128)(2,1)S(1)}, bf16[4,32,1536]{2,0,1:T(4,128)(2,1)S(1)}, u32[]{:S(2)}, u32[]{:S(2)}) %collective-permute-start.6) | collective-permute-done | bytes 393248 | tf_op jit(solution)/shard_map/ppermute | solution.py:17
  58.2 7.2 %all-to-all-start.1 = ((bf16[8,64,128]{2,1,0:T(8,128)(2,1)}), bf16[8,64,128]{2,1,0:T(8,128)(2,1)S(1)}, u32[]{:S(2)}, u32[]{:S(2)}) async-start(bf16[8,64,128]{2,1,0:T(8,128)(2,1)} %add_convert_fusion.2), calls=%async_computation.2 | async-start | bytes 262144 | tf_op jit(solution)/shard_map/all_to_all | solution.py:49
  65.5 2.5 %convolution_convert_fusion.2 = bf16[512,512]{1,0:T(8,128)(2,1)S(1)} fusion(bf16[512,1536]{1,0:T(8,128)(2,1)S(1)} %bitcast.172, bf16[1536,512]{1,0:T(8,128)(2,1)} %all-gather.2.cloned.1.call-done), kind=kOutput, calls=%fused_computation.12 | convolution fusion | flops 805568512 | bytes 3670016 | tf_op jit(solution)/shard_map/dot_general | solution.py:96
  68.0 2.4 %convolution_convert_fusion.1 = bf16[512,512]{1,0:T(8,128)(2,1)S(1)} fusion(bf16[512,1536]{1,0:T(8,128)(2,1)} %collective-permute-done.7, bf16[1536,512]{1,0:T(8,128)(2,1)S(1)} %copy-done.20), kind=kOutput, calls=%fused_computation.11 | convolution fusion | flops 805568512 | bytes 3670016 | tf_op jit(solution)/shard_map/dot_general | solution.py:96
  75.3 3.5 %all-to-all-start.2 = ((bf16[4,2,4,32,512]{4,3,2,1,0:T(8,128)(2,1)}), bf16[4,2,4,32,512]{4,3,2,1,0:T(8,128)(2,1)S(1)}, u32[]{:S(2)}, u32[]{:S(2)}) async-start(bf16[4,2,4,32,512]{4,3,2,1,0:T(8,128)(2,1)} %broadcast_in_dim.197), calls=%async_computation.3 | async-start | bytes 2097152 | tf_op jit(solution)/shard_map/all_to_all | solution.py:115
  79.6 21.5 %all-to-all-done.2 = bf16[4,2,4,32,512]{4,3,2,1,0:T(8,128)(2,1)S(1)} async-done(((bf16[4,2,4,32,512]{4,3,2,1,0:T(8,128)(2,1)}), bf16[4,2,4,32,512]{4,3,2,1,0:T(8,128)(2,1)S(1)}, u32[]{:S(2)}, u32[]{:S(2)}) %all-to-all-start.2) | async-done | bytes 1048608 | tf_op jit(solution)/shard_map/all_to_all | solution.py:115
  102.2 2.1 %fusion.18 = f32[512,1536]{1,0:T(8,128)S(1)} fusion(bf16[512,1536]{1,0:T(8,128)(2,1)S(1)} %bitcast.173, bf16[2,512,512]{2,1,0:T(8,128)(2,1)} %bitcast.176), kind=kOutput, calls=%fused_computation.44 | convolution fusion | flops 805306368 | bytes 5242880 | tf_op jit(solution)/shard_map/dot_general | solution.py:127
  104.4 2.4 %fusion = bf16[512,1536]{1,0:T(8,128)(2,1)S(1)} fusion(f32[512,1536]{1,0:T(8,128)S(1)} %fusion.18, bf16[512,1536]{1,0:T(8,128)(2,1)} %collective-permute-done.7, bf16[2,512,512]{2,1,0:T(8,128)(2,1)S(1)} %bitcast.177), kind=kOutput, calls=%fused_computation.3 | convolution fusion | flops 806879232 | bytes 6815744 | tf_op jit(solution)/shard_map/dot_general | solution.py:129
  108.8 2.2 %convolution_convert_fusion = bf16[512,1536]{1,0:T(8,128)(2,1)} fusion(bf16[1536,512]{1,0:T(8,128)(2,1)S(1)} %copy-done.21, bf16[2,512,512]{2,1,0:T(8,128)(2,1)S(1)} %bitcast.178), kind=kOutput, calls=%fused_computation.2 | convolution fusion | flops 806092800 | bytes 3670016 | tf_op jit(solution)/shard_map/dot_general | solution.py:123
  116.4 6.8 %all-to-all-start.3 = ((bf16[8,64,128]{2,1,0:T(8,128)(2,1)}), bf16[8,64,128]{2,1,0:T(8,128)(2,1)S(1)}, u32[]{:S(2)}, u32[]{:S(2)}) async-start(bf16[8,64,128]{2,1,0:T(8,128)(2,1)} %bitcast.34), calls=%async_computation.4 | async-start | bytes 262144 | tf_op jit(solution)/shard_map/all_to_all | solution.py:28
  123.3 2.9 %fusion.1 = bf16[512,1536]{1,0:T(8,128)(2,1)S(1)} fusion(bf16[512,1536]{1,0:T(8,128)(2,1)} %collective-permute-done.8, bf16[1536,512]{1,0:T(8,128)(2,1)} %all-gather.2.cloned.1.call-done, bf16[2,512,512]{2,1,0:T(8,128)(2,1)S(1)} %bitcast.179), kind=kOutput, calls=%fused_computation.4 | convolution fusion | flops 807665664 | bytes 5242880 | tf_op jit(solution)/shard_map/dot_general | solution.py:123
  129.4 3.8 %all-to-all-done.3 = bf16[8,64,128]{2,1,0:T(8,128)(2,1)S(1)} async-done(((bf16[8,64,128]{2,1,0:T(8,128)(2,1)}), bf16[8,64,128]{2,1,0:T(8,128)(2,1)S(1)}, u32[]{:S(2)}, u32[]{:S(2)}) %all-to-all-start.3) | async-done | bytes 131104 | tf_op jit(solution)/shard_map/all_to_all | solution.py:28
  134.8 4.1 %collective-permute-done.9 = bf16[80,128]{1,0:T(8,128)(2,1)S(1)} collective-permute-done((bf16[80,128]{1,0:T(8,128)(2,1)S(1)}, bf16[80,128]{1,0:T(8,128)(2,1)S(1)}, u32[]{:S(2)}, u32[]{:S(2)}) %collective-permute-start.9) | collective-permute-done | bytes 20512 | tf_op jit(solution)/shard_map/ppermute | solution.py:44
  141.8 4.1 %all-to-all-start.4 = ((bf16[8,64,128]{2,1,0:T(8,128)(2,1)}), bf16[8,64,128]{2,1,0:T(8,128)(2,1)S(1)}, u32[]{:S(2)}, u32[]{:S(2)}) async-start(bf16[8,64,128]{2,1,0:T(8,128)(2,1)} %add_convert_fusion.1), calls=%async_computation.5 | async-start | bytes 262144 | tf_op jit(solution)/shard_map/all_to_all | solution.py:49
  146.0 2.6 %collective-permute-done.10 = bf16[128,1536]{1,0:T(8,128)(2,1)} collective-permute-done((bf16[128,1536]{1,0:T(8,128)(2,1)S(1)}, bf16[128,1536]{1,0:T(8,128)(2,1)}, u32[]{:S(2)}, u32[]{:S(2)}) %collective-permute-start.10) | collective-permute-done | bytes 393248 | tf_op jit(solution)/shard_map/ppermute | solution.py:17
  153.9 3.1 %collective-permute-start.14 = (bf16[48,1536]{1,0:T(8,128)(2,1)S(1)}, bf16[48,1536]{1,0:T(8,128)(2,1)S(1)}, u32[]{:S(2)}, u32[]{:S(2)}) collective-permute-start(bf16[48,1536]{1,0:T(8,128)(2,1)S(1)} %get-tuple-element.82), channel_id=1, source_target_pairs={{0,128},{64,192},{128,0},{192,64},{1,129},{65,193},{129,1},{193,65... | collective-permute-start | bytes 442376 | tf_op jit(solution)/shard_map/ppermute | solution.py:17
  159.2 2.2 %collective-permute-done.14 = bf16[48,1536]{1,0:T(8,128)(2,1)S(1)} collective-permute-done((bf16[48,1536]{1,0:T(8,128)(2,1)S(1)}, bf16[48,1536]{1,0:T(8,128)(2,1)S(1)}, u32[]{:S(2)}, u32[]{:S(2)}) %collective-permute-start.14) | collective-permute-done | bytes 147488 | tf_op jit(solution)/shard_map/ppermute | solution.py:17
  (163 shorter events, 50.4 us)
Async XLA Ops:
  7.2 47.4 %all-gather.2.cloned.1.call-start = ((), (), s32[]{:S(2)}) async-start(), calls=%async_computation.7 | async-start | bytes 1769472 | tf_op jit(solution)/shard_map/all_gather | solution.py:63
  13.7 15.6 %collective-permute-start.1 = (bf16[32,1536]{1,0:T(8,128)(2,1)S(1)}, bf16[32,1536]{1,0:T(8,128)(2,1)S(1)}, u32[]{:S(2)}, u32[]{:S(2)}) collective-permute-start(bf16[32,1536]{1,0:T(8,128)(2,1)S(1)} %bitcast.206), channel_id=1, source_target_pairs={{0,192},{64,0},{128,64},{192,128},{1,193},{65,1},{129,65},{193,129... | collective-permute-start | bytes 294920 | tf_op jit(solution)/shard_map/ppermute | solution.py:17
  16.9 12.7 %collective-permute-start.2 = (bf16[32,1536]{1,0:T(8,128)(2,1)S(1)}, bf16[32,1536]{1,0:T(8,128)(2,1)S(1)}, u32[]{:S(2)}, u32[]{:S(2)}) collective-permute-start(bf16[32,1536]{1,0:T(8,128)(2,1)S(1)} %bitcast.208), channel_id=1, source_target_pairs={{0,128},{64,192},{128,0},{192,64},{1,129},{65,193},{129,1},{193,65... | collective-permute-start | bytes 294920 | tf_op jit(solution)/shard_map/ppermute | solution.py:17
  17.6 12.1 %collective-permute-start.3 = (bf16[32,1536]{1,0:T(8,128)(2,1)S(1)}, bf16[32,1536]{1,0:T(8,128)(2,1)S(1)}, u32[]{:S(2)}, u32[]{:S(2)}) collective-permute-start(bf16[32,1536]{1,0:T(8,128)(2,1)S(1)} %bitcast.210), channel_id=1, source_target_pairs={{0,64},{64,128},{128,192},{192,0},{1,65},{65,129},{129,193},{193,1... | collective-permute-start | bytes 294920 | tf_op jit(solution)/shard_map/ppermute | solution.py:17
  20.8 18.7 %all-to-all-start = ((bf16[8,80,128]{2,1,0:T(8,128)(2,1)}), bf16[8,80,128]{2,1,0:T(8,128)(2,1)S(1)}, u32[]{:S(2)}, u32[]{:S(2)}) async-start(bf16[8,80,128]{2,1,0:T(8,128)(2,1)} %pad_maximum_fusion.6), calls=%async_computation | async-start | bytes 327680 | tf_op jit(solution)/shard_map/all_to_all | solution.py:28
  32.7 18.4 %collective-permute-start.4 = (bf16[4,32,1536]{2,0,1:T(4,128)(2,1)S(1)}, bf16[4,32,1536]{2,0,1:T(4,128)(2,1)S(1)}, u32[]{:S(2)}, u32[]{:S(2)}) collective-permute-start(bf16[4,32,1536]{2,0,1:T(4,128)(2,1)S(1)} %constant_dynamic-slice_fusion.1), channel_id=1, source_target_pairs={{0,6},{2,0},{4,2},{6,4},{1,7},{3,1},{5,3},{7,5},{8,14},{10,8},{12,... | collective-permute-start | bytes 1179656 | tf_op jit(solution)/shard_map/ppermute | solution.py:17
  35.5 15.5 %collective-permute-start.5 = (bf16[4,32,1536]{2,0,1:T(4,128)(2,1)S(1)}, bf16[4,32,1536]{2,0,1:T(4,128)(2,1)S(1)}, u32[]{:S(2)}, u32[]{:S(2)}) collective-permute-start(bf16[4,32,1536]{2,0,1:T(4,128)(2,1)S(1)} %constant_dynamic-slice_fusion.1), channel_id=1, source_target_pairs={{0,4},{2,6},{4,0},{6,2},{1,5},{3,7},{5,1},{7,3},{8,12},{10,14},{12... | collective-permute-start | bytes 1179656 | tf_op jit(solution)/shard_map/ppermute | solution.py:17
  36.3 18.3 %collective-permute-start.6 = (bf16[4,32,1536]{2,0,1:T(4,128)(2,1)S(1)}, bf16[4,32,1536]{2,0,1:T(4,128)(2,1)S(1)}, u32[]{:S(2)}, u32[]{:S(2)}) collective-permute-start(bf16[4,32,1536]{2,0,1:T(4,128)(2,1)S(1)} %constant_dynamic-slice_fusion.1), channel_id=1, source_target_pairs={{0,2},{2,4},{4,6},{6,0},{1,3},{3,5},{5,7},{7,1},{8,10},{10,12},{12... | collective-permute-start | bytes 1179656 | tf_op jit(solution)/shard_map/ppermute | solution.py:17
  43.5 5.4 %collective-permute-start = (bf16[80,128]{1,0:T(8,128)(2,1)S(1)}, bf16[80,128]{1,0:T(8,128)(2,1)S(1)}, u32[]{:S(2)}, u32[]{:S(2)}) collective-permute-start(bf16[80,128]{1,0:T(8,128)(2,1)S(1)} %concatenate.30), channel_id=1, source_target_pairs={{0,64},{64,128},{128,192},{1,65},{65,129},{129,193},{2,66},{66,130... | collective-permute-start | bytes 61448 | tf_op jit(solution)/shard_map/ppermute | solution.py:44
  56.4 11.6 %collective-permute-start.7 = (bf16[512,1536]{1,0:T(8,128)(2,1)S(1)}, bf16[512,1536]{1,0:T(8,128)(2,1)}, u32[]{:S(2)}, u32[]{:S(2)}) collective-permute-start(bf16[512,1536]{1,0:T(8,128)(2,1)S(1)} %bitcast.171), channel_id=1, source_target_pairs={{0,1},{1,0},{2,3},{3,2},{4,5},{5,4},{6,7},{7,6},{8,9},{9,8},{10,11... | collective-permute-start | bytes 4718600 | tf_op jit(solution)/shard_map/ppermute | solution.py:94
  58.2 15.0 %all-to-all-start.1 = ((bf16[8,64,128]{2,1,0:T(8,128)(2,1)}), bf16[8,64,128]{2,1,0:T(8,128)(2,1)S(1)}, u32[]{:S(2)}, u32[]{:S(2)}) async-start(bf16[8,64,128]{2,1,0:T(8,128)(2,1)} %add_convert_fusion.2), calls=%async_computation.2 | async-start | bytes 262144 | tf_op jit(solution)/shard_map/all_to_all | solution.py:49
  65.5 36.8 %reduce-scatter.3.cloned.1.call-start = ((), (), s32[]{:S(2)}) async-start(), calls=%async_computation.8 | async-start | bytes 1310720 | tf_op jit(solution)/shard_map/reduce_scatter | solution.py:117
  75.3 25.9 %all-to-all-start.2 = ((bf16[4,2,4,32,512]{4,3,2,1,0:T(8,128)(2,1)}), bf16[4,2,4,32,512]{4,3,2,1,0:T(8,128)(2,1)S(1)}, u32[]{:S(2)}, u32[]{:S(2)}) async-start(bf16[4,2,4,32,512]{4,3,2,1,0:T(8,128)(2,1)} %broadcast_in_dim.197), calls=%async_computation.3 | async-start | bytes 2097152 | tf_op jit(solution)/shard_map/all_to_all | solution.py:115
  78.8 71.9 %reduce-scatter.5.cloned.1.call-start = ((), (), s32[]{:S(2)}) async-start(), calls=%async_computation.9 | async-start | bytes 1769472 | tf_op jit(solution)/shard_map/reduce_scatter | solution.py:147
  111.0 5.4 %collective-permute-start.8 = (bf16[512,1536]{1,0:T(8,128)(2,1)}, bf16[512,1536]{1,0:T(8,128)(2,1)}, u32[]{:S(2)}, u32[]{:S(2)}) collective-permute-start(bf16[512,1536]{1,0:T(8,128)(2,1)} %convolution_convert_fusion), channel_id=1, source_target_pairs={{0,1},{1,0},{2,3},{3,2},{4,5},{5,4},{6,7},{7,6},{8,9},{9,8},{10,11... | collective-permute-start | bytes 4718600 | tf_op jit(solution)/shard_map/ppermute | solution.py:148
  116.4 16.7 %all-to-all-start.3 = ((bf16[8,64,128]{2,1,0:T(8,128)(2,1)}), bf16[8,64,128]{2,1,0:T(8,128)(2,1)S(1)}, u32[]{:S(2)}, u32[]{:S(2)}) async-start(bf16[8,64,128]{2,1,0:T(8,128)(2,1)} %bitcast.34), calls=%async_computation.4 | async-start | bytes 262144 | tf_op jit(solution)/shard_map/all_to_all | solution.py:28
  127.3 18.6 %collective-permute-start.12 = (bf16[128,1536]{1,0:T(8,128)(2,1)}, bf16[128,1536]{1,0:T(8,128)(2,1)}, u32[]{:S(2)}, u32[]{:S(2)}) collective-permute-start(bf16[128,1536]{1,0:T(8,128)(2,1)} %get-tuple-element.75), channel_id=1, source_target_pairs={{0,6},{2,0},{4,2},{6,4},{1,7},{3,1},{5,3},{7,5},{8,14},{10,8},{12,... | collective-permute-start | bytes 1179656 | tf_op jit(solution)/shard_map/ppermute | solution.py:17
  127.6 18.4 %collective-permute-start.11 = (bf16[128,1536]{1,0:T(8,128)(2,1)}, bf16[128,1536]{1,0:T(8,128)(2,1)}, u32[]{:S(2)}, u32[]{:S(2)}) collective-permute-start(bf16[128,1536]{1,0:T(8,128)(2,1)} %get-tuple-element.76), channel_id=1, source_target_pairs={{0,4},{2,6},{4,0},{6,2},{1,5},{3,7},{5,1},{7,3},{8,12},{10,14},{12... | collective-permute-start | bytes 1179656 | tf_op jit(solution)/shard_map/ppermute | solution.py:17
  128.4 20.2 %collective-permute-start.10 = (bf16[128,1536]{1,0:T(8,128)(2,1)S(1)}, bf16[128,1536]{1,0:T(8,128)(2,1)}, u32[]{:S(2)}, u32[]{:S(2)}) collective-permute-start(bf16[128,1536]{1,0:T(8,128)(2,1)S(1)} %get-tuple-element.74), channel_id=1, source_target_pairs={{0,2},{2,4},{4,6},{6,0},{1,3},{3,5},{5,7},{7,1},{8,10},{10,12},{12... | collective-permute-start | bytes 1179656 | tf_op jit(solution)/shard_map/ppermute | solution.py:17
  133.2 5.7 %collective-permute-start.9 = (bf16[80,128]{1,0:T(8,128)(2,1)S(1)}, bf16[80,128]{1,0:T(8,128)(2,1)S(1)}, u32[]{:S(2)}, u32[]{:S(2)}) collective-permute-start(bf16[80,128]{1,0:T(8,128)(2,1)S(1)} %concatenate.34), channel_id=1, source_target_pairs={{64,0},{128,64},{192,128},{65,1},{129,65},{193,129},{66,2},{130,66... | collective-permute-start | bytes 61448 | tf_op jit(solution)/shard_map/ppermute | solution.py:44
  141.8 11.8 %all-to-all-start.4 = ((bf16[8,64,128]{2,1,0:T(8,128)(2,1)}), bf16[8,64,128]{2,1,0:T(8,128)(2,1)S(1)}, u32[]{:S(2)}, u32[]{:S(2)}) async-start(bf16[8,64,128]{2,1,0:T(8,128)(2,1)} %add_convert_fusion.1), calls=%async_computation.5 | async-start | bytes 262144 | tf_op jit(solution)/shard_map/all_to_all | solution.py:49
  153.6 5.6 %collective-permute-start.13 = (bf16[48,1536]{1,0:T(8,128)(2,1)S(1)}, bf16[48,1536]{1,0:T(8,128)(2,1)S(1)}, u32[]{:S(2)}, u32[]{:S(2)}) collective-permute-start(bf16[48,1536]{1,0:T(8,128)(2,1)S(1)} %get-tuple-element.83), channel_id=1, source_target_pairs={{0,192},{64,0},{128,64},{192,128},{1,193},{65,1},{129,65},{193,129... | collective-permute-start | bytes 442376 | tf_op jit(solution)/shard_map/ppermute | solution.py:17
  153.9 7.5 %collective-permute-start.14 = (bf16[48,1536]{1,0:T(8,128)(2,1)S(1)}, bf16[48,1536]{1,0:T(8,128)(2,1)S(1)}, u32[]{:S(2)}, u32[]{:S(2)}) collective-permute-start(bf16[48,1536]{1,0:T(8,128)(2,1)S(1)} %get-tuple-element.82), channel_id=1, source_target_pairs={{0,128},{64,192},{128,0},{192,64},{1,129},{65,193},{129,1},{193,65... | collective-permute-start | bytes 442376 | tf_op jit(solution)/shard_map/ppermute | solution.py:17
  157.0 6.4 %collective-permute-start.15 = (bf16[48,1536]{1,0:T(8,128)(2,1)S(1)}, bf16[48,1536]{1,0:T(8,128)(2,1)S(1)}, u32[]{:S(2)}, u32[]{:S(2)}) collective-permute-start(bf16[48,1536]{1,0:T(8,128)(2,1)S(1)} %get-tuple-element.81), channel_id=1, source_target_pairs={{0,64},{64,128},{128,192},{192,0},{1,65},{65,129},{129,193},{193,1... | collective-permute-start | bytes 442376 | tf_op jit(solution)/shard_map/ppermute | solution.py:17
  (22 other events, 119.4 us)
Sparse Core Ops, SparseCore 0:
  9.8 43.7 all-gather.1
  71.7 28.6 reduce-scatter.2
  111.9 38.7 reduce-scatter.4
